TPU v7x, 32 devices: a whole 2x2x4 slice. The times are simulated.
32 devices in a mesh: dp: 32 (over z, y, x, core).
Axes of the slice: x: 2, y: 2, z: 4, core: 2. Of those that a mesh axis runs over, the one named last changes fastest.
Arguments:
- params: float32 [1774080], P('dp')
- images: bfloat16 [256, 197, 384], P('dp'), may hold values from -6 to 6
- cotangent: bfloat16 [256, 197, 384], P('dp'), may hold values from -6 to 6
- live: int32 [32], P('dp'), may hold values from 1 to 8, as said below
Outputs:
- layer_out: bfloat16 [256, 197, 384], P('dp')
- input_grad: bfloat16 [256, 197, 384], P('dp')
- flat_parameter_gradient: float32 [1774080], P('dp')
Inputs may be any that keep to these rules, and one draw needn't show every extreme that they name: The first live[d] of device d's 8 slots hold images; every draw has a device with all 8 slots occupied.
All inputs are finite; a program needn't handle non-finite values.
Results may differ from a plain program's by a relative error of at most 0.0098.
Values may be sent and summed in bfloat16 or wider, within the bound.
A program may use at most 192 MiB of HBM per device.

v0:
```python
import functools

import jax
import jax.numpy as jnp
from jax import lax
from jax.experimental import pallas as pl
from jax.experimental.pallas import tpu as pltpu
from jax.sharding import PartitionSpec as P

D = 384
HEADS = 6
FF = 1536
HD = D // HEADS
PAIRS = HEADS // 2
EPS = 1e-06
LANES = 128
BF = jnp.bfloat16
F32 = jnp.float32

ROW_QKV = 2
ROW_OUT = 2 + 3 * D + 2
ROW_UP = ROW_OUT + D + 3
ROW_BUP = ROW_UP + FF
ROW_DOWN = ROW_BUP + FF // D
ROW_BDOWN = ROW_DOWN + FF
ROWS = ROW_BDOWN + 1
VEC_ROWS = (0, 1, ROW_OUT - 2, ROW_OUT - 1, ROW_UP - 3, ROW_UP - 2, ROW_UP - 1, ROW_BDOWN)
G1, S1, BQ, BV, BO, G2, S2, BD = range(8)

GROUP = 4
CHUNK = 512


def up_to(value, unit):
    return (value + unit - 1) // unit * unit


def nt(a, b):
    return lax.dot_general(a, b, (((1,), (1,)), ((), ())), preferred_element_type=F32)


def tn(a, b):
    return lax.dot_general(a, b, (((0,), (0,)), ((), ())), preferred_element_type=F32)


def nn(a, b):
    return jnp.dot(a, b, preferred_element_type=F32)


def norm_stats(values):
    center = values - jnp.mean(values, axis=-1, keepdims=True)
    inv = lax.rsqrt(jnp.mean(center * center, axis=-1, keepdims=True) + EPS)
    return center * inv, inv


def norm_back(grad_out, hat, inv, gain):
    g = grad_out * gain
    return inv * (
        g
        - jnp.mean(g, axis=-1, keepdims=True)
        - hat * jnp.mean(g * hat, axis=-1, keepdims=True)
    )


def colsum(v):
    return jnp.sum(v, axis=0, keepdims=True)


def matrices():
    return (
        (0, D, 9, ROW_QKV),
        (1, D, 3, ROW_OUT),
        (2, D, 12, ROW_UP),
        (3, FF, 3, ROW_DOWN),
    )


def layer_kernel(
    n, shard, tok, tokp,
    live_ref, gath_ref, img_ref, cot_ref,
    out_ref, din_ref, grad_ref,
    buf, wqkv, wout, wup, wdn, vec, bup,
    gqkv, gout, gup, gdn, gvec, gbup,
    x_s, dout_s, attn_s, qkv_s, probs_s, mixed_s, dmix_s, dqkv_s,
):
    step = pl.program_id(0)
    window = gath_ref.shape[1]
    weights = (wqkv, wout, wup, wdn)
    grads = (gqkv, gout, gup, gdn)

    @pl.when(step == 0)
    def _():
        for d in range(n):
            first, shift = divmod(shard * d, LANES)
            rows = (shift + shard + LANES - 1) // LANES
            piece = gath_ref[d].astype(F32)
            if d > 0 and shift:
                seam = buf[first : first + 1, :] + piece[0:1]
                buf[first : first + rows, :] = piece[:rows]
                buf[first : first + 1, :] = seam
            else:
                buf[first : first + rows, :] = piece[:rows]
        for k, rows, blocks, start in matrices():
            for b in range(blocks):
                weights[k][:, b * LANES : (b + 1) * LANES] = buf[
                    pl.ds(3 * start + b, rows, blocks), :
                ].astype(BF)
        for i, r in enumerate(VEC_ROWS):
            for c in range(3):
                vec[i : i + 1, c * LANES : (c + 1) * LANES] = buf[3 * r + c : 3 * r + c + 1, :]
        for c in range(FF // LANES):
            bup[:, c * LANES : (c + 1) * LANES] = buf[3 * ROW_BUP + c : 3 * ROW_BUP + c + 1, :]
        for ref in (*grads, gvec, gbup, x_s, dout_s):
            ref[...] = jnp.zeros_like(ref)

    def param(i):
        return vec[i : i + 1, :]

    def add_vec(i, value):
        gvec[i : i + 1, :] += value

    live = live_ref[0]
    masks = [(step * GROUP + g < live).astype(F32) for g in range(GROUP)]
    for g in range(GROUP):
        x_s[g * tokp : g * tokp + tok, :] = img_ref[g].astype(F32)
        dout_s[g * tokp : g * tokp + tok, :] = cot_ref[g].astype(F32) * masks[g]

    hat1, _ = norm_stats(x_s[...])
    attn_s[...] = (hat1 * param(G1) + param(S1)).astype(BF)
    attn_in = attn_s[...]
    for j, bias in enumerate((BQ, None, BV)):
        part = nn(attn_in, wqkv[:, j * D : (j + 1) * D])
        if bias is not None:
            part = part + param(bias)
        qkv_s[:, j * D : (j + 1) * D] = part.astype(BF)

    lane = lax.broadcasted_iota(jnp.int32, (1, LANES), 1)
    low = lane < HD
    low_b = low.astype(BF)
    high_b = 1 - low_b
    key_ok = lax.broadcasted_iota(jnp.int32, (1, tokp), 1) < tok

    def views(t):
        g, p = t // PAIRS, t % PAIRS
        rows = pl.ds(pl.multiple_of(g * tokp, 16), tokp)
        return rows, [pl.ds(pl.multiple_of(j * D + p * LANES, LANES), LANES) for j in range(3)]

    def stack(v):
        return jnp.concatenate([v * low_b, v * high_b], axis=0)

    def attend(t, carry):
        rows, (cq, ck, cv) = views(t)
        q, k, v = qkv_s[rows, cq], qkv_s[rows, ck], qkv_s[rows, cv]
        s = nt(stack(q), k) * (HD**-0.5)
        s = jnp.where(key_ok, s, -1e30)
        e = jnp.exp(s - jnp.max(s, axis=-1, keepdims=True))
        probs = e * (1.0 / jnp.sum(e, axis=-1, keepdims=True))
        probs_s[t] = probs
        mixed = nn(probs.astype(BF), v)
        mixed_s[rows, cq] = jnp.where(low, mixed[:tokp], mixed[tokp:]).astype(BF)
        return carry

    lax.fori_loop(0, GROUP * PAIRS, attend, 0)

    hidden = x_s[...] + nn(mixed_s[...], wout[...]) + param(BO)
    hat2, inv2 = norm_stats(hidden)
    ffn_in = (hat2 * param(G2) + param(S2)).astype(BF)
    dout = dout_s[...]
    dout_b = dout.astype(BF)
    add_vec(BD, colsum(dout))
    result = hidden + param(BD)
    dn2 = jnp.zeros_like(hidden)
    for c in range(FF // CHUNK):
        cols = slice(c * CHUNK, (c + 1) * CHUNK)
        pre = nn(ffn_in, wup[:, cols]) + bup[:, cols]
        cumul = 0.5 * (1.0 + lax.erf(pre * 0.7071067811865476))
        act = (pre * cumul).astype(BF)
        result = result + nn(act, wdn[cols, :])
        gdn[cols, :] += tn(act, dout_b)
        density = jnp.exp(-0.5 * pre * pre) * 0.3989422804014327
        dpre = nt(dout_b, wdn[cols, :]) * (cumul + pre * density)
        gbup[:, cols] += colsum(dpre)
        dpre_b = dpre.astype(BF)
        gup[:, cols] += tn(ffn_in, dpre_b)
        dn2 = dn2 + nt(dpre_b, wup[:, cols])
    for g in range(GROUP):
        out_ref[g] = (result[g * tokp : g * tokp + tok] * masks[g]).astype(BF)

    add_vec(G2, colsum(dn2 * hat2))
    add_vec(S2, colsum(dn2))
    dhidden = dout + norm_back(dn2, hat2, inv2, param(G2))
    dout_s[...] = dhidden
    dhidden_b = dhidden.astype(BF)
    add_vec(BO, colsum(dhidden))
    gout[...] += tn(mixed_s[...], dhidden_b)
    dmix_s[...] = nt(dhidden_b, wout[...]).astype(BF)

    def attend_back(t, carry):
        rows, (cq, ck, cv) = views(t)
        q, k, v = qkv_s[rows, cq], qkv_s[rows, ck], qkv_s[rows, cv]
        dm = stack(dmix_s[rows, cq])
        probs = probs_s[t]
        dprobs = nt(dm, v)
        delta = jnp.sum(probs * dprobs, axis=-1, keepdims=True)
        ds = (probs * (dprobs - delta) * (HD**-0.5)).astype(BF)
        dvalue = tn(probs.astype(BF), dm)
        dq = nn(ds, k)
        dquery = jnp.where(low, dq[:tokp], dq[tokp:])
        dkey = tn(ds, stack(q))
        gvec[BQ : BQ + 1, cq] += colsum(dquery)
        gvec[BV : BV + 1, cq] += colsum(dvalue)
        dqkv_s[rows, cq] = dquery.astype(BF)
        dqkv_s[rows, ck] = dkey.astype(BF)
        dqkv_s[rows, cv] = dvalue.astype(BF)
        return carry

    lax.fori_loop(0, GROUP * PAIRS, attend_back, 0)

    attn_in = attn_s[...]
    dn1 = jnp.zeros_like(hidden)
    for j in range(3):
        cols = slice(j * D, (j + 1) * D)
        part = dqkv_s[:, cols]
        gqkv[:, cols] += tn(attn_in, part)
        dn1 = dn1 + nt(part, wqkv[:, cols])
    hat1, inv1 = norm_stats(x_s[...])
    add_vec(G1, colsum(dn1 * hat1))
    add_vec(S1, colsum(dn1))
    dinput = dout_s[...] + norm_back(dn1, hat1, inv1, param(G1))
    for g in range(GROUP):
        din_ref[g] = dinput[g * tokp : g * tokp + tok].astype(BF)
        dout_s[g * tokp + tok : (g + 1) * tokp, :] = jnp.zeros((tokp - tok, D), F32)

    @pl.when(step == pl.num_programs(0) - 1)
    def _():
        for k, rows, blocks, start in matrices():
            for b in range(blocks):
                buf[pl.ds(3 * start + b, rows, blocks), :] = grads[k][
                    :, b * LANES : (b + 1) * LANES
                ]
        for i, r in enumerate(VEC_ROWS):
            for c in range(3):
                buf[3 * r + c : 3 * r + c + 1, :] = gvec[i : i + 1, c * LANES : (c + 1) * LANES]
        for c in range(FF // LANES):
            buf[3 * ROW_BUP + c : 3 * ROW_BUP + c + 1, :] = gbup[:, c * LANES : (c + 1) * LANES]
        tail = buf.shape[0] - 3 * ROWS
        buf[3 * ROWS :, :] = jnp.zeros((tail, LANES), F32)
        for d in range(n):
            first = shard * d // LANES
            grad_ref[d] = buf[first : first + window, :].astype(grad_ref.dtype)


def run_layer(n, shard, window, live, gathered, images, cotangent):
    slots, tok, _ = images.shape
    tokp = up_to(tok, 16)
    rows = GROUP * tokp
    buf_rows = up_to(max(shard * (n - 1) // LANES + window, 3 * ROWS) + 8, 8)
    block = pl.BlockSpec((GROUP, tok, D), lambda i: (i, 0, 0))
    whole = pl.BlockSpec(memory_space=pltpu.VMEM)
    VM = pltpu.VMEM
    return pl.pallas_call(
        functools.partial(layer_kernel, n, shard, tok, tokp),
        grid=(slots // GROUP,),
        in_specs=[pl.BlockSpec(memory_space=pltpu.SMEM), whole, block, block],
        out_specs=[block, block, whole],
        out_shape=[
            jax.ShapeDtypeStruct(images.shape, BF),
            jax.ShapeDtypeStruct(images.shape, BF),
            jax.ShapeDtypeStruct((n, window, LANES), BF),
        ],
        scratch_shapes=[
            VM((buf_rows, LANES), F32),
            VM((D, 3 * D), BF), VM((D, D), BF), VM((D, FF), BF), VM((FF, D), BF),
            VM((8, D), F32), VM((1, FF), F32),
            VM((D, 3 * D), F32), VM((D, D), F32), VM((D, FF), F32), VM((FF, D), F32),
            VM((8, D), F32), VM((1, FF), F32),
            VM((rows, D), F32), VM((rows, D), F32), VM((rows, D), BF),
            VM((rows, 3 * D), BF), VM((GROUP * PAIRS, 2 * tokp, tokp), F32),
            VM((rows, D), BF), VM((rows, D), BF), VM((rows, 3 * D), BF),
        ],
        compiler_params=pltpu.CompilerParams(
            dimension_semantics=("arbitrary",), vmem_limit_bytes=63 * 1024 * 1024
        ),
        name="layer",
    )(live, gathered, images, cotangent)


PARTS = 4
MESH = pl.DeviceIdType.MESH


def flip(index, mask, bits):
    for b in range(bits):
        if mask >> b & 1:
            index = index + (1 - 2 * (index // (1 << b) % 2)) * (1 << b)
    return index


def part_orders(bits):
    near = list(range(bits))
    swapped = near[:1] + near[2:3] + near[1:2] + near[3:]
    orders = [near, swapped]
    for order in (near, swapped):
        orders.append(order[:2] + order[3:4] + order[2:3] + order[4:])
    return orders


def mask_of(k, rest):
    return sum(1 << b for i, b in enumerate(rest) if k >> (len(rest) - 1 - i) & 1)


def greet(me, bits):
    barrier = pltpu.get_barrier_semaphore()
    for b in range(bits):
        pl.semaphore_signal(
            barrier, inc=1, device_id=(flip(me, 1 << b, bits),), device_id_type=MESH
        )
    pl.semaphore_wait(barrier, bits)


def gather_kernel(bits, x_ref, out_ref, send_sem, recv_sem):
    me = lax.axis_index("dp")
    window = x_ref.shape[0]
    part = window // PARTS
    orders = [order[::-1] for order in part_orders(bits)]
    greet(me, bits)
    sends = []

    def copy(p, source, slot, to, first):
        rows = pl.ds(p * part, part)
        return pltpu.make_async_remote_copy(
            src_ref=x_ref.at[rows] if first else out_ref.at[source, rows],
            dst_ref=out_ref.at[source, rows],
            send_sem=send_sem.at[p, slot],
            recv_sem=recv_sem.at[p, slot],
            device_id=(to,),
            device_id_type=MESH,
        )

    def start(p, s):
        order = orders[p]
        to = flip(me, 1 << order[s], bits)
        for k in range(1 << s):
            source = flip(me, mask_of(k, order[:s]), bits)
            c = copy(p, source, (1 << s) - 1 + k, to, k == 0)
            c.start()
            sends.append(c)

    def arrive(p, s):
        order = orders[p]
        to = flip(me, 1 << order[s], bits)
        for k in range(1 << s):
            source = flip(me, mask_of(k, order[:s]) | 1 << order[s], bits)
            copy(p, source, (1 << s) - 1 + k, to, False).wait_recv()

    for p in range(PARTS):
        start(p, 0)
    out_ref[me] = x_ref[...]
    for s in range(bits):
        for p in range(PARTS):
            arrive(p, s)
            if s + 1 < bits:
                start(p, s + 1)
    for c in sends:
        c.wait_send()


def gather(x, n):
    bits = n.bit_length() - 1
    return pl.pallas_call(
        functools.partial(gather_kernel, bits),
        out_shape=jax.ShapeDtypeStruct((n,) + x.shape, x.dtype),
        in_specs=[pl.BlockSpec(memory_space=pltpu.VMEM)],
        out_specs=pl.BlockSpec(memory_space=pltpu.VMEM),
        scratch_shapes=[
            pltpu.SemaphoreType.DMA((PARTS, n - 1)),
            pltpu.SemaphoreType.DMA((PARTS, n - 1)),
        ],
        compiler_params=pltpu.CompilerParams(
            collective_id=1, has_side_effects=True, vmem_limit_bytes=32 * 1024 * 1024
        ),
        name="gather",
    )(x)


def reduce_kernel(bits, g_ref, out_ref, acc, recv, send_sem, recv_sem, first_send, first_recv):
    me = lax.axis_index("dp")
    half = 1 << (bits - 1)
    part = g_ref.shape[1] // PARTS
    orders = part_orders(bits)
    greet(me, bits)
    sends = []

    def first_copy(p, k):
        order = orders[p]
        block = flip(me, mask_of(k, order[1:]) | 1 << order[0], bits)
        return pltpu.make_async_remote_copy(
            src_ref=g_ref.at[block, pl.ds(p * part, part)],
            dst_ref=recv.at[p, k],
            send_sem=first_send.at[p, k],
            recv_sem=first_recv.at[p, k],
            device_id=(flip(me, 1 << order[0], bits),),
            device_id_type=MESH,
        )

    def later_copy(p, s):
        count = half >> s
        base = 2 * half - 2 * count
        return pltpu.make_async_remote_copy(
            src_ref=acc.at[p, pl.ds(count, count)],
            dst_ref=recv.at[p, pl.ds(base, count)],
            send_sem=send_sem.at[p, s],
            recv_sem=recv_sem.at[p, s],
            device_id=(flip(me, 1 << orders[p][s], bits),),
            device_id_type=MESH,
        )

    for p in range(PARTS):
        for k in reversed(range(half)):
            c = first_copy(p, k)
            c.start()
            sends.append(c)
    for s in range(bits):
        count = half >> s
        base = 2 * half - 2 * count
        for p in range(PARTS):
            rows = pl.ds(p * part, part)
            if s == 0:
                for k in reversed(range(half)):
                    first_copy(p, k).wait_recv()
                    own = flip(me, mask_of(k, orders[p][1:]), bits)
                    total = g_ref[own, rows].astype(F32) + recv[p, k].astype(F32)
                    acc[p, k] = total.astype(BF)
                    if k == half // 2:
                        c = later_copy(p, 1)
                        c.start()
                        sends.append(c)
                continue
            later_copy(p, s).wait_recv()
            for k in reversed(range(count)):
                total = acc[p, k].astype(F32) + recv[p, base + k].astype(F32)
                if s + 1 == bits:
                    out_ref[rows, :] = total
                else:
                    acc[p, k] = total.astype(BF)
                    if k == count // 2:
                        c = later_copy(p, s + 1)
                        c.start()
                        sends.append(c)
    for c in sends:
        c.wait_send()


def reduce_windows(grads, n):
    bits = n.bit_length() - 1
    window = grads.shape[1]
    return pl.pallas_call(
        functools.partial(reduce_kernel, bits),
        out_shape=jax.ShapeDtypeStruct((window, LANES), F32),
        in_specs=[pl.BlockSpec(memory_space=pltpu.VMEM)],
        out_specs=pl.BlockSpec(memory_space=pltpu.VMEM),
        scratch_shapes=[
            pltpu.VMEM((PARTS, n // 2, window // PARTS, LANES), BF),
            pltpu.VMEM((PARTS, n, window // PARTS, LANES), BF),
            pltpu.SemaphoreType.DMA((PARTS, bits)),
            pltpu.SemaphoreType.DMA((PARTS, bits)),
            pltpu.SemaphoreType.DMA((PARTS, n // 2)),
            pltpu.SemaphoreType.DMA((PARTS, n // 2)),
        ],
        compiler_params=pltpu.CompilerParams(
            collective_id=2, has_side_effects=True, vmem_limit_bytes=40 * 1024 * 1024
        ),
        name="reduce",
    )(grads)


def shards(params, images, cotangent, live):
    n = lax.axis_size("dp")
    assert n & (n - 1) == 0 and n >= 4
    shard = params.shape[0]
    window = up_to((shard + 2 * LANES - 2) // LANES, 16 * PARTS)
    me = lax.axis_index("dp")
    shift = (shard % LANES) * me % LANES
    padded = jnp.pad(params, (0, window * LANES - shard))
    moved = jnp.roll(padded, shift).astype(BF).reshape(window, LANES)
    gathered = gather(moved, n)
    out, din, grads = run_layer(n, shard, window, live, gathered, images, cotangent)
    mine = reduce_windows(grads, n)
    flat = lax.dynamic_slice(mine.reshape(-1), (shift,), (shard,))
    return out, din, flat


def solution(mesh):
    return jax.shard_map(
        shards,
        mesh=mesh,
        in_specs=(P("dp"), P("dp", None, None), P("dp", None, None), P("dp")),
        out_specs=(P("dp", None, None), P("dp", None, None), P("dp")),
        check_vma=False,
    )
```

profile of v0, /device:TPU:0, one launch (start us, length us, event | category | flops | bytes accessed | tf_op | source)
XLA Modules:
  0.0 147.3 jit_solution(6927577442880554095)
XLA Ops:
  1.3 1.0 pad.4
  2.3 0.5 fusion.2.x_ref
  2.8 0.0 copy-start.3
  2.8 2.6 %copy.7.img_ref = bf16[8,197,384]{2,1,0:T(8,128)(2,1)} copy(bf16[8,197,384]{2,0,1:T(8,128)(2,1)} %param.5) | data formatting | bytes 2420736 | tf_op args[1]
  5.4 0.0 copy-done.3
  5.4 1.3 copy.8.cot_ref
  6.7 32.0 %gather.1.gath_ref = bf16[32,448,128]{2,1,0:T(8,128)(2,1)S(1)} custom-call(bf16[448,128]{1,0:T(8,128)(2,1)S(1)} %fusion.2.x_ref), custom_call_target="tpu_custom_call" | custom-call | tf_op jit(solution)/shard_map/gather/pallas_call | solution.py:370
  38.7 0.0 copy-start
  38.7 1.8 %copy-done = bf16[32,448,128]{2,1,0:T(8,128)(2,1)} copy-done((bf16[32,448,128]{2,1,0:T(8,128)(2,1)}, bf16[32,448,128]{2,1,0:T(8,128)(2,1)S(1)}, u32[]{:S(2)}) %copy-start) | copy-done | bytes 3670040
  40.5 69.8 %layer.1 = (bf16[8,197,384]{2,1,0:T(8,128)(2,1)}, bf16[8,197,384]{2,1,0:T(8,128)(2,1)}, bf16[32,448,128]{2,1,0:T(8,128)(2,1)}) custom-call(s32[1]{0:T(128)S(6)} %copy.11.live_ref, bf16[32,448,128]{2,1,0:T(8,128)(2,1)} %copy-done, bf16[8,197,384]{2,1,0:T(8,128)(2,1)} %copy.7.img_ref, bf16[8,197,384]{2,1,0:T(8,128)(2,1)} %copy.8.cot_ref), custom_call_target="tpu_custom_call" | custom-call | tf_op jit(solution)/shard_map/layer/pallas_call | solution.py:261
  110.3 2.5 %copy.9 = bf16[8,197,384]{2,0,1:T(8,128)(2,1)} copy(bf16[8,197,384]{2,1,0:T(8,128)(2,1)} %get-tuple-element.9) | data formatting | bytes 2420736
  112.8 0.0 copy-start.1
  112.8 2.0 %copy-done.1 = bf16[32,448,128]{2,1,0:T(8,128)(2,1)S(1)} copy-done((bf16[32,448,128]{2,1,0:T(8,128)(2,1)S(1)}, bf16[32,448,128]{2,1,0:T(8,128)(2,1)}, u32[]{:S(2)}) %copy-start.1) | copy-done | bytes 3670040
  114.8 0.0 copy-start.2
  114.8 30.5 %reduce.1 = f32[448,128]{1,0:T(8,128)S(1)} custom-call(bf16[32,448,128]{2,1,0:T(8,128)(2,1)S(1)} %copy-done.1), custom_call_target="tpu_custom_call" | custom-call | tf_op jit(solution)/shard_map/reduce/pallas_call | solution.py:457
  145.3 0.8 dynamic_slice.8
  146.1 0.0 copy-done.2
  146.1 1.2 copy.10
Async XLA Ops:
  2.8 2.6 %copy-start.3 = (bf16[8,197,384]{2,0,1:T(8,128)(2,1)S(1)}, bf16[8,197,384]{2,0,1:T(8,128)(2,1)}, u32[]{:S(2)}) copy-start(bf16[8,197,384]{2,0,1:T(8,128)(2,1)} %param.6) | copy-start | bytes 3631108
  38.7 1.8 %copy-start = (bf16[32,448,128]{2,1,0:T(8,128)(2,1)}, bf16[32,448,128]{2,1,0:T(8,128)(2,1)S(1)}, u32[]{:S(2)}) copy-start(bf16[32,448,128]{2,1,0:T(8,128)(2,1)S(1)} %gather.1.gath_ref) | copy-start | bytes 11010052
  112.8 2.0 %copy-start.1 = (bf16[32,448,128]{2,1,0:T(8,128)(2,1)S(1)}, bf16[32,448,128]{2,1,0:T(8,128)(2,1)}, u32[]{:S(2)}) copy-start(bf16[32,448,128]{2,1,0:T(8,128)(2,1)} %get-tuple-element.8.g_ref) | copy-start | bytes 11010052
  114.8 31.3 %copy-start.2 = (bf16[8,197,384]{2,1,0:T(8,128)(2,1)S(1)}, bf16[8,197,384]{2,1,0:T(8,128)(2,1)}, u32[]{:S(2)}) copy-start(bf16[8,197,384]{2,1,0:T(8,128)(2,1)} %get-tuple-element.10) | copy-start | bytes 3631108
where the time goes:
time: 148 us; the launch traced here: 147 us
  Pallas kernels  132 us (89%)
  local copies, waits for them, and re-layouts  13.1 us (9%)
    pallas_call x1, Pallas kernels, run_layer(): pl.pallas_call(functools.partial(layer_kernel, n, shard, tok, tokp), grid...  69.8 us
    pallas_call x1, Pallas kernels, gather(): pl.pallas_call(functools.partial(gather_kernel, bits), out_shape=jax.Shap...  32 us
    pallas_call x1, Pallas kernels, reduce_windows(): pl.pallas_call(functools.partial(reduce_kernel, bits), out_shape=jax.Shap...  30.5 us
    unnamed x12, local copies, waits for them, and re-layouts  11.4 us

commit v1 on v0

v1 whole, which is shorter than its diff:
```python
import functools

import jax
import jax.numpy as jnp
from jax import lax
from jax.experimental import pallas as pl
from jax.experimental.pallas import tpu as pltpu
from jax.sharding import PartitionSpec as P

D = 384
HEADS = 6
FF = 1536
HD = D // HEADS
PAIRS = HEADS // 2
EPS = 1e-06
LANES = 128
BF = jnp.bfloat16
F32 = jnp.float32

ROW_QKV = 2
ROW_OUT = 2 + 3 * D + 2
ROW_UP = ROW_OUT + D + 3
ROW_BUP = ROW_UP + FF
ROW_DOWN = ROW_BUP + FF // D
ROW_BDOWN = ROW_DOWN + FF
ROWS = ROW_BDOWN + 1
VEC_ROWS = (0, 1, ROW_OUT - 2, ROW_OUT - 1, ROW_UP - 3, ROW_UP - 2, ROW_UP - 1, ROW_BDOWN)
G1, S1, BQ, BV, BO, G2, S2, BD = range(8)

CHUNK = 256
PARTS = 4
UNROLL = 2
BLOCKS = 4
MESH = pl.DeviceIdType.MESH


def up_to(value, unit):
    return (value + unit - 1) // unit * unit


def nt(a, b):
    return lax.dot_general(a, b, (((1,), (1,)), ((), ())), preferred_element_type=F32)


def tn(a, b):
    return lax.dot_general(a, b, (((0,), (0,)), ((), ())), preferred_element_type=F32)


def nn(a, b):
    return jnp.dot(a, b, preferred_element_type=F32)


def norm_stats(values):
    center = values - jnp.mean(values, axis=-1, keepdims=True)
    inv = lax.rsqrt(jnp.mean(center * center, axis=-1, keepdims=True) + EPS)
    return center * inv, inv


def norm_back(grad_out, hat, inv, gain):
    g = grad_out * gain
    return inv * (
        g
        - jnp.mean(g, axis=-1, keepdims=True)
        - hat * jnp.mean(g * hat, axis=-1, keepdims=True)
    )


def colsum(v):
    return jnp.sum(v, axis=0, keepdims=True)


def part_orders(bits):
    near = list(range(bits))
    swapped = near[:1] + near[2:3] + near[1:2] + near[3:]
    orders = [near, swapped]
    for order in (near, swapped):
        orders.append(order[:2] + order[3:4] + order[2:3] + order[4:])
    return orders


def matrices():
    return (
        (0, D, 9, ROW_QKV),
        (1, D, 3, ROW_OUT),
        (2, D, 12, ROW_UP),
        (3, FF, 3, ROW_DOWN),
    )


def step_kernel(
    n, shard, slots, tok, tokp,
    live_ref, mine_ref, img_hbm, cot_hbm,
    out_ref, din_ref, flat_ref,
    gath, recv, buf, wqkv, wout, wup, wdn, vec, bup, gvec,
    img_v, cot_v, stage, x_s, dout_s, attn_s, qkv_s, probs_s, mixed_s,
    hat_s, inv_s, res_s, dn2_s, ffn_s,
    load_sem, gsend, grecv, rsend, rrecv,
):
    bits = n.bit_length() - 1
    me = lax.axis_index("dp")
    window = mine_ref.shape[0]
    part = window // PARTS
    weights = (wqkv, wout, wup, wdn)
    early = -(-3 * ROW_OUT * LANES // shard)
    delta = [(1 - 2 * (me // (1 << b) % 2)) * (1 << b) for b in range(bits)]
    r_orders = part_orders(bits)
    g_orders = [order[::-1] for order in r_orders]

    def in_wave(block, wave):
        return block < early if wave == 0 else block >= early

    def spread(k, dims):
        return sum(((k // (1 << i)) % 2) * delta[b] for i, b in enumerate(dims))

    def each(count, body):
        if count == 1:
            body(0)
            return

        def step(k, carry):
            body(k)
            return carry

        lax.fori_loop(0, count, step, 0)

    def gather_copy(p, s, k, source, first):
        rows = pl.ds(p * part, part)
        slot = (1 << s) - 1 + k
        return pltpu.make_async_remote_copy(
            src_ref=mine_ref.at[rows] if first else gath.at[source, rows],
            dst_ref=gath.at[source, rows],
            send_sem=gsend.at[p, slot],
            recv_sem=grecv.at[p, slot],
            device_id=(me + delta[g_orders[p][s]],),
            device_id_type=MESH,
        )

    def gather_start(p, s, wave):
        def body(k):
            source = me + spread(k, g_orders[p][:s])

            @pl.when(in_wave(source, wave))
            def _():
                gather_copy(p, s, k, source, s == 0).start()

        each(1 << s, body)

    def gather_sent(p, s, wave):
        def body(k):
            source = me + spread(k, g_orders[p][:s])

            @pl.when(in_wave(source, wave))
            def _():
                gather_copy(p, s, k, source, s == 0).wait_send()

        each(1 << s, body)

    def gather_arrive(p, s, wave):
        def body(k):
            source = me + delta[g_orders[p][s]] + spread(k, g_orders[p][:s])

            @pl.when(in_wave(source, wave))
            def _():
                gather_copy(p, s, k, source, False).wait_recv()

        each(1 << s, body)

    def gather_round(s, wave):
        for p in range(PARTS):
            gather_arrive(p, s, wave)
            if s + 1 < bits:
                gather_start(p, s + 1, wave)

    def reduce_copy(p, s, k, block):
        slot = n - (n >> s) + k
        return pltpu.make_async_remote_copy(
            src_ref=gath.at[block, pl.ds(p * part, part)],
            dst_ref=recv.at[p, slot],
            send_sem=rsend.at[p, slot],
            recv_sem=rrecv.at[p, slot],
            device_id=(me + delta[r_orders[p][s]],),
            device_id_type=MESH,
        )

    def reduce_start(p, s, wave):
        order = r_orders[p]

        def body(k):
            block = me + delta[order[s]] + spread(k, order[s + 1 :])

            @pl.when(in_wave(block, wave))
            def _():
                reduce_copy(p, s, k, block).start()

        each(n >> (s + 1), body)

    def reduce_sent(p, s, wave):
        order = r_orders[p]

        def body(k):
            block = me + delta[order[s]] + spread(k, order[s + 1 :])

            @pl.when(in_wave(block, wave))
            def _():
                reduce_copy(p, s, k, block).wait_send()

        each(n >> (s + 1), body)

    def reduce_absorb(p, s, wave):
        rows = pl.ds(p * part, part)

        def body(k):
            block = me + spread(k, r_orders[p][s + 1 :])

            @pl.when(in_wave(block, wave))
            def _():
                reduce_copy(p, s, k, block).wait_recv()
                slot = n - (n >> s) + k
                total = gath[block, rows].astype(F32) + recv[p, slot].astype(F32)
                if s + 1 == bits:
                    flat_ref[rows, :] = total
                else:
                    gath[block, rows] = total.astype(BF)

        each(n >> (s + 1), body)

    def reduce_round(s, wave):
        for p in range(PARTS):
            reduce_absorb(p, s, wave)
            if s + 1 < bits:
                reduce_start(p, s + 1, wave)

    def unpack(blocks):
        for d in blocks:
            first, shift = divmod(shard * d, LANES)
            rows = (shift + shard + LANES - 1) // LANES
            piece = gath[d].astype(F32)
            if d > 0 and shift:
                seam = buf[first : first + 1, :] + piece[0:1]
                buf[first : first + rows, :] = piece[:rows]
                buf[first : first + 1, :] = seam
            else:
                buf[first : first + rows, :] = piece[:rows]

    def load_matrix(k, rows, blocks, start):
        for b in range(blocks):
            weights[k][:, b * LANES : (b + 1) * LANES] = buf[
                pl.ds(3 * start + b, rows, blocks), :
            ].astype(BF)

    def load_vectors(indices):
        for i in indices:
            r = VEC_ROWS[i]
            for c in range(3):
                vec[i : i + 1, c * LANES : (c + 1) * LANES] = buf[3 * r + c : 3 * r + c + 1, :]

    def put_vector(i, value):
        r = VEC_ROWS[i]
        for c in range(3):
            buf[3 * r + c : 3 * r + c + 1, :] = value[:, c * LANES : (c + 1) * LANES]

    def pack(blocks):
        for d in blocks:
            first = shard * d // LANES
            gath[d] = buf[first : first + window, :].astype(BF)

    def param(i):
        return vec[i : i + 1, :]

    loads = [
        pltpu.make_async_copy(img_hbm, img_v, load_sem.at[0]),
        pltpu.make_async_copy(cot_hbm, cot_v, load_sem.at[1]),
    ]
    for c in loads:
        c.start()
    barrier = pltpu.get_barrier_semaphore()
    for b in range(bits):
        pl.semaphore_signal(barrier, inc=1, device_id=(me + delta[b],), device_id_type=MESH)
    pl.semaphore_wait(barrier, bits)
    for wave in range(2):
        for p in range(PARTS):
            gather_start(p, 0, wave)
    gath[me] = mine_ref[...]

    def scatter_rows(source, target, scales):
        for c in range(3):
            stage[c] = source[:, c * LANES : (c + 1) * LANES].astype(F32)
        target[...] = jnp.zeros_like(target)
        for g in range(slots):
            for c in range(3):
                cols = slice(c * LANES, (c + 1) * LANES)
                v = stage[c, pl.ds(g, tok, slots), :]
                if scales is not None:
                    v = v * scales[g]
                target[g * tokp : g * tokp + tok, cols] = v.astype(BF)

    live = live_ref[0]
    masks = [(g < live).astype(F32) for g in range(slots)]
    loads[0].wait()
    scatter_rows(img_v, x_s, None)
    gather_round(0, 0)
    loads[1].wait()
    scatter_rows(cot_v, dout_s, masks)
    for s in range(1, bits):
        gather_round(s, 0)
    unpack(range(early))
    load_matrix(*matrices()[0])
    load_vectors((G1, S1, BQ, BV))
    gvec[...] = jnp.zeros_like(gvec)

    height = x_s.shape[0] // BLOCKS
    bias = jnp.concatenate([param(BQ), jnp.zeros((1, D), F32), param(BV)], axis=1)

    def band(i):
        return pl.ds(pl.multiple_of(i * height, 16), height)

    def project(i, carry):
        hat1, _ = norm_stats(x_s[band(i), :].astype(F32))
        attn_in = (hat1 * param(G1) + param(S1)).astype(BF)
        attn_s[band(i), :] = attn_in
        qkv_s[band(i), :] = (nn(attn_in, wqkv[...]) + bias).astype(BF)
        return carry

    lax.fori_loop(0, BLOCKS, project, 0)

    lane = lax.broadcasted_iota(jnp.int32, (1, LANES), 1)
    low = lane < HD
    low_b = low.astype(BF)
    high_b = 1 - low_b
    key_ok = lax.broadcasted_iota(jnp.int32, (1, tokp), 1) < tok

    def views(t):
        g, p = t // PAIRS, t % PAIRS
        rows = pl.ds(pl.multiple_of(g * tokp, 16), tokp)
        return rows, [pl.ds(pl.multiple_of(j * D + p * LANES, LANES), LANES) for j in range(3)]

    def stack(v, scale=1.0):
        return jnp.concatenate([v * (low_b * scale), v * (high_b * scale)], axis=0)

    def attend(t):
        rows, (cq, ck, cv) = views(t)
        q, k, v = qkv_s[rows, cq], qkv_s[rows, ck], qkv_s[rows, cv]
        s = nt(stack(q, HD**-0.5), k)
        s = jnp.where(key_ok, s, -1e30)
        e = jnp.exp(s - jnp.max(s, axis=-1, keepdims=True))
        probs = (e * (1.0 / jnp.sum(e, axis=-1, keepdims=True))).astype(BF)
        probs_s[t] = probs
        mixed = nn(probs, v)
        mixed_s[rows, cq] = jnp.where(low, mixed[:tokp], mixed[tokp:]).astype(BF)

    tiles = slots * PAIRS
    trips = tiles // UNROLL

    def forward(i, carry):
        for s in range(bits):
            @pl.when(i == (s * trips) // bits)
            def _():
                gather_round(s, 1)

        for u in range(UNROLL):
            attend(i * UNROLL + u)
        return carry

    lax.fori_loop(0, trips, forward, 0)
    for wave in range(2):
        for p in range(PARTS):
            for s in range(bits):
                gather_sent(p, s, wave)
    unpack(range(early, n))
    for m in matrices()[1:]:
        load_matrix(*m)
    load_vectors((BO, G2, S2, BD))
    for c in range(FF // LANES):
        bup[:, c * LANES : (c + 1) * LANES] = buf[3 * ROW_BUP + c : 3 * ROW_BUP + c + 1, :]
    tail = buf.shape[0] - 3 * ROWS
    buf[3 * ROWS :, :] = jnp.zeros((tail, LANES), F32)

    def add_vector(i, value):
        gvec[i : i + 1, :] += value

    def second_norm(i, carry):
        rows = band(i)
        hidden = x_s[rows, :].astype(F32) + nn(mixed_s[rows, :], wout[...]) + param(BO)
        hat2, inv2 = norm_stats(hidden)
        ffn_s[rows, :] = (hat2 * param(G2) + param(S2)).astype(BF)
        hat_s[rows, :] = hat2
        inv_s[rows, :] = inv2
        res_s[rows, :] = hidden + param(BD)
        dn2_s[rows, :] = jnp.zeros((height, D), F32)
        add_vector(BD, colsum(dout_s[rows, :].astype(F32)))
        return carry

    lax.fori_loop(0, BLOCKS, second_norm, 0)

    def feed(c, carry):
        cols = pl.ds(pl.multiple_of(c * CHUNK, CHUNK), CHUNK)
        ffn_in = ffn_s[...]
        dout_b = dout_s[...]
        pre = nn(ffn_in, wup[:, cols]) + bup[:, cols]
        cumul = 0.5 * (1.0 + lax.erf(pre * 0.7071067811865476))
        act = (pre * cumul).astype(BF)
        res_s[...] += nn(act, wdn[cols, :])
        grad = tn(act, dout_b)
        for b in range(3):
            buf[pl.ds(3 * ROW_DOWN + 3 * CHUNK * c + b, CHUNK, 3), :] = grad[
                :, b * LANES : (b + 1) * LANES
            ]
        density = jnp.exp(-0.5 * pre * pre) * 0.3989422804014327
        dpre = nt(dout_b, wdn[cols, :]) * (cumul + pre * density)
        total = colsum(dpre)
        dpre_b = dpre.astype(BF)
        grad = tn(ffn_in, dpre_b)
        for b in range(CHUNK // LANES):
            lanes = slice(b * LANES, (b + 1) * LANES)
            at = c * (CHUNK // LANES) + b
            buf[pl.ds(3 * ROW_UP + at, D, FF // LANES), :] = grad[:, lanes]
            buf[pl.ds(3 * ROW_BUP + at, 1), :] = total[:, lanes]
        dn2_s[...] += nt(dpre_b, wup[:, cols])
        return carry

    lax.fori_loop(0, FF // CHUNK, feed, 0)

    def gather_back(value, source_ref):
        for g in range(slots):
            for c in range(3):
                cols = slice(c * LANES, (c + 1) * LANES)
                v = source_ref[g * tokp : g * tokp + tok, cols]
                if value is not None:
                    v = v * value[g]
                stage[c, pl.ds(g, tok, slots), :] = v

    def emit_rows(target):
        for c in range(3):
            target[:, c * LANES : (c + 1) * LANES] = stage[c].astype(BF)

    def second_norm_back(i, carry):
        rows = band(i)
        hat2 = hat_s[rows, :]
        dn2 = dn2_s[rows, :]
        add_vector(G2, colsum(dn2 * hat2))
        add_vector(S2, colsum(dn2))
        dhidden = dout_s[rows, :].astype(F32) + norm_back(dn2, hat2, inv_s[rows, :], param(G2))
        dn2_s[rows, :] = dhidden
        dhidden_b = dhidden.astype(BF)
        add_vector(BO, colsum(dhidden))
        dout_s[rows, :] = dhidden_b
        ffn_s[rows, :] = nt(dhidden_b, wout[...]).astype(BF)
        return carry

    lax.fori_loop(0, BLOCKS, second_norm_back, 0)
    grad = tn(mixed_s[...], dout_s[...])
    for b in range(3):
        buf[pl.ds(3 * ROW_OUT + b, D, 3), :] = grad[:, b * LANES : (b + 1) * LANES]
    for i in (BO, G2, S2, BD):
        put_vector(i, gvec[i : i + 1, :])
    pack(range(early, n))
    for p in range(PARTS):
        reduce_start(p, 0, 1)
    gather_back(masks, res_s)
    emit_rows(img_v)
    out_copy = pltpu.make_async_copy(img_v, out_ref, load_sem.at[2])
    out_copy.start()

    def attend_back(t):
        rows, (cq, ck, cv) = views(t)
        q, k, v = qkv_s[rows, cq], qkv_s[rows, ck], qkv_s[rows, cv]
        dm = stack(ffn_s[rows, cq])
        probs = probs_s[t]
        wide = probs.astype(F32)
        dprobs = nt(dm, v)
        delta_p = jnp.sum(wide * dprobs, axis=-1, keepdims=True)
        ds = (wide * (dprobs - delta_p)).astype(BF)
        dvalue = tn(probs, dm)
        dq = nn(ds, k)
        dquery = jnp.where(low, dq[:tokp], dq[tokp:]) * (HD**-0.5)
        dkey = tn(ds, stack(q, HD**-0.5))
        gvec[BQ : BQ + 1, cq] += colsum(dquery)
        gvec[BV : BV + 1, cq] += colsum(dvalue)
        qkv_s[rows, cq] = dquery.astype(BF)
        qkv_s[rows, ck] = dkey.astype(BF)
        qkv_s[rows, cv] = dvalue.astype(BF)

    def backward(i, carry):
        for s in range(bits):
            @pl.when(i == ((s + 1) * trips) // (bits + 1))
            def _():
                reduce_round(s, 1)

        for u in range(UNROLL):
            attend_back(i * UNROLL + u)
        return carry

    lax.fori_loop(0, trips, backward, 0)

    def first_norm_back(i, carry):
        rows = band(i)
        dn1 = nt(qkv_s[rows, :], wqkv[...])
        hat1, inv1 = norm_stats(x_s[rows, :].astype(F32))
        add_vector(G1, colsum(dn1 * hat1))
        add_vector(S1, colsum(dn1))
        res_s[rows, :] = dn2_s[rows, :] + norm_back(dn1, hat1, inv1, param(G1))
        return carry

    lax.fori_loop(0, BLOCKS, first_norm_back, 0)

    def grad_qkv(c, carry):
        cols = pl.ds(pl.multiple_of(c * LANES, LANES), LANES)
        grad = tn(attn_s[:, cols], qkv_s[...])
        for b in range(9):
            at = 3 * ROW_QKV + 9 * LANES * c + b
            buf[pl.ds(at, LANES, 9), :] = grad[:, b * LANES : (b + 1) * LANES]
        return carry

    lax.fori_loop(0, 3, grad_qkv, 0)
    for i in (G1, S1, BQ, BV):
        put_vector(i, gvec[i : i + 1, :])
    pack(range(early))
    for p in range(PARTS):
        reduce_start(p, 0, 0)
    gather_back(None, res_s)
    emit_rows(cot_v)
    din_copy = pltpu.make_async_copy(cot_v, din_ref, load_sem.at[3])
    din_copy.start()
    for s in range(bits):
        reduce_round(s, 0)
    for wave in range(2):
        for p in range(PARTS):
            for s in range(bits):
                reduce_sent(p, s, wave)
    out_copy.wait()
    din_copy.wait()


def run_step(n, shard, window, live, mine, images, cotangent):
    tok, slots, _ = images.shape
    tokp = up_to(tok, 16)
    rows = slots * tokp
    flat = (slots * tok, D)
    buf_rows = up_to(max(shard * (n - 1) // LANES + window, 3 * ROWS) + 8, 8)
    whole = pl.BlockSpec(memory_space=pltpu.VMEM)
    apart = pl.BlockSpec(memory_space=pl.ANY)
    VM = pltpu.VMEM
    sems = pltpu.SemaphoreType.DMA((PARTS, n - 1))
    out, din, mine = pl.pallas_call(
        functools.partial(step_kernel, n, shard, slots, tok, tokp),
        in_specs=[pl.BlockSpec(memory_space=pltpu.SMEM), whole, apart, apart],
        out_specs=[apart, apart, whole],
        out_shape=[
            jax.ShapeDtypeStruct(flat, BF),
            jax.ShapeDtypeStruct(flat, BF),
            jax.ShapeDtypeStruct((window, LANES), F32),
        ],
        scratch_shapes=[
            VM((n, window, LANES), BF),
            VM((PARTS, n - 1, window // PARTS, LANES), BF),
            VM((buf_rows, LANES), F32),
            VM((D, 3 * D), BF), VM((D, D), BF), VM((D, FF), BF), VM((FF, D), BF),
            VM((8, D), F32), VM((1, FF), F32), VM((8, D), F32),
            VM(flat, BF), VM(flat, BF), VM((3, slots * tok, LANES), F32),
            VM((rows, D), BF), VM((rows, D), BF), VM((rows, D), BF),
            VM((rows, 3 * D), BF), VM((slots * PAIRS, 2 * tokp, tokp), BF),
            VM((rows, D), BF),
            VM((rows, D), F32), VM((rows, 1), F32), VM((rows, D), F32), VM((rows, D), F32), VM((rows, D), BF),
            pltpu.SemaphoreType.DMA((4,)), sems, sems, sems, sems,
        ],
        compiler_params=pltpu.CompilerParams(
            collective_id=1, has_side_effects=True, vmem_limit_bytes=67043328
        ),
        name="step",
    )(live, mine, images.reshape(flat), cotangent.reshape(flat))
    return out.reshape(tok, slots, D), din.reshape(tok, slots, D), mine


def shards(params, images, cotangent, live):
    n = lax.axis_size("dp")
    assert n & (n - 1) == 0 and n >= 4
    shard = params.shape[0]
    window = up_to((shard + 2 * LANES - 2) // LANES, 16 * PARTS)
    me = lax.axis_index("dp")
    shift = (shard % LANES) * me % LANES
    padded = jnp.pad(params, (0, window * LANES - shard))
    moved = jnp.roll(padded, shift).astype(BF).reshape(window, LANES)
    images, cotangent = (jnp.transpose(a, (1, 0, 2)) for a in (images, cotangent))
    out, din, mine = run_step(n, shard, window, live, moved, images, cotangent)
    out, din = (jnp.transpose(a, (1, 0, 2)) for a in (out, din))
    flat = lax.dynamic_slice(mine.reshape(-1), (shift,), (shard,))
    return out, din, flat


def solution(mesh):
    return jax.shard_map(
        shards,
        mesh=mesh,
        in_specs=(P("dp"), P("dp", None, None), P("dp", None, None), P("dp")),
        out_specs=(P("dp", None, None), P("dp", None, None), P("dp")),
        check_vma=False,
    )
```

time: 148 us -> 159 us (1.074)
  Pallas kernels: 132 us -> 150 us
  local copies, waits for them, and re-layouts: 13.1 us -> 6.26 us
    pallas_call x3 -> x1, Pallas kernels: 132 us -> 150 us  [run_step(): pl.pallas_call(functools.partial(step_kernel, n, shard, slots, tok, tokp)...]
    unnamed x12 -> x4, local copies, waits for them, and re-layouts: 11.4 us -> 3.55 us
where the time goes in v1:
time: 159 us
  Pallas kernels  150 us (94%)
  local copies, waits for them, and re-layouts  6.26 us (4%)
    pallas_call x1, Pallas kernels, run_step(): pl.pallas_call(functools.partial(step_kernel, n, shard, slots, tok, tokp)...  150 us
    unnamed x4, local copies, waits for them, and re-layouts  3.55 us

profile of v1, /device:TPU:0, one launch (start us, length us, event | category | flops | bytes accessed | tf_op | source)
XLA Modules:
  0.0 158.8 jit_solution(13862092593896016344)
XLA Ops:
  1.3 1.0 pad.4
  2.3 1.2 fusion.2.mine_ref
  3.4 150.0 %step.1 = (bf16[1576,384]{1,0:T(8,128)(2,1)}, bf16[1576,384]{1,0:T(8,128)(2,1)}, f32[448,128]{1,0:T(8,128)}) custom-call(s32[1]{0:T(128)S(6)} %copy.9.live_ref, bf16[448,128]{1,0:T(8,128)(2,1)} %fusion.2.mine_ref, bf16[1576,384]{1,0:T(8,128)(2,1)} %bitcast.17, bf16[1576,384]{1,0:T(8,128)(2,1)} %bitcast.18), custom_call_target="tpu_custom_call" | custom-call | tf_op jit(solution)/shard_map/step/pallas_call | solution.py:544
  153.4 1.8 %dynamic_slice.8 = f32[55440]{0:T(1024)} dynamic-slice(f32[57344]{0:T(1024)} %bitcast.19, s32[]{:T(128)S(6)} %select_n.25), dynamic_slice_sizes={55440} | dynamic-slice | bytes 443524 | tf_op jit(solution)/shard_map/dynamic_slice | solution.py:586
  155.2 0.0 copy-start
  155.2 2.5 %copy.10 = bf16[8,197,384]{2,0,1:T(8,128)(2,1)} copy(bf16[8,197,384]{2,0,1:T(8,128)(2,1)} %bitcast.16) | data formatting | bytes 2420736
  157.7 0.0 copy-done
  157.7 1.0 copy.11
Async XLA Ops:
  155.2 2.5 %copy-start = (bf16[1576,384]{1,0:T(8,128)(2,1)S(1)}, bf16[1576,384]{1,0:T(8,128)(2,1)}, u32[]{:S(2)}) copy-start(bf16[1576,384]{1,0:T(8,128)(2,1)} %get-tuple-element.7) | copy-start | bytes 3631108

commit v2 on v1

--- a/solution.py
+++ b/solution.py
@@ -69,13 +69,25 @@
     return jnp.sum(v, axis=0, keepdims=True)
 
 
-def part_orders(bits):
-    near = list(range(bits))
-    swapped = near[:1] + near[2:3] + near[1:2] + near[3:]
-    orders = [near, swapped]
-    for order in (near, swapped):
-        orders.append(order[:2] + order[3:4] + order[2:3] + order[4:])
-    return orders
+def low_orders(low_bits):
+    near = list(range(low_bits))[::-1]
+    swapped = near[1:2] + near[:1] + near[2:] if low_bits > 2 else near
+    return [near, swapped] * (PARTS // 2)
+
+
+def place(low, order):
+    return sum((low >> b & 1) << i for i, b in enumerate(order))
+
+
+def plan(n, shard):
+    needed = -(-3 * ROW_OUT * LANES // shard)
+    low_bits = max(needed.bit_length() - 1, 1)
+    if needed > (1 << low_bits) + 1:
+        low_bits += 1
+    low_bits = min(low_bits, n.bit_length() - 2)
+    head = 3 * ROW_OUT - (shard << low_bits) // LANES
+    assert head <= 16
+    return low_bits, max(head, 0)
 
 
 def matrices():
@@ -91,156 +103,243 @@
     n, shard, slots, tok, tokp,
     live_ref, mine_ref, img_hbm, cot_hbm,
     out_ref, din_ref, flat_ref,
-    gath, recv, buf, wqkv, wout, wup, wdn, vec, bup, gvec,
+    gath, recv, recv_up, head_v, head_in, buf, wqkv, wout, wup, wdn, vec, bup, gvec,
     img_v, cot_v, stage, x_s, dout_s, attn_s, qkv_s, probs_s, mixed_s,
     hat_s, inv_s, res_s, dn2_s, ffn_s,
-    load_sem, gsend, grecv, rsend, rrecv,
+    load_sem, gu_send, gu_recv, gl_send, gl_recv,
+    ru_send, ru_recv, rl_send, rl_recv, gh_send, gh_recv, rh_send, rh_recv,
 ):
     bits = n.bit_length() - 1
     me = lax.axis_index("dp")
     window = mine_ref.shape[0]
     part = window // PARTS
     weights = (wqkv, wout, wup, wdn)
-    early = -(-3 * ROW_OUT * LANES // shard)
     delta = [(1 - 2 * (me // (1 << b) % 2)) * (1 << b) for b in range(bits)]
-    r_orders = part_orders(bits)
-    g_orders = [order[::-1] for order in r_orders]
-
-    def in_wave(block, wave):
-        return block < early if wave == 0 else block >= early
-
-    def spread(k, dims):
-        return sum(((k // (1 << i)) % 2) * delta[b] for i, b in enumerate(dims))
-
-    def each(count, body):
-        if count == 1:
-            body(0)
-            return
-
-        def step(k, carry):
-            body(k)
-            return carry
-
-        lax.fori_loop(0, count, step, 0)
-
-    def gather_copy(p, s, k, source, first):
-        rows = pl.ds(p * part, part)
-        slot = (1 << s) - 1 + k
+    bit = [me // (1 << b) % 2 for b in range(bits)]
+    e, head = plan(n, shard)
+    near_count, uppers = 1 << e, n >> e
+    up = me // near_count
+    near_me = me % near_count
+    orders = low_orders(e)
+    spots = [sum(bit[b] * (1 << i) for i, b in enumerate(order)) for order in orders]
+    waves = (pl.ds(0, 1), pl.ds(1, uppers - 1))
+
+    def peer(j):
+        return me + sum(delta[e + b] for b in range(bits - e) if j >> b & 1)
+
+    def fixed(p, i):
+        return sum(bit[b] * (1 << k) for k, b in enumerate(orders[p]) if k >= i)
+
+    def remote(src, dst, send, recv_at, to):
         return pltpu.make_async_remote_copy(
-            src_ref=mine_ref.at[rows] if first else gath.at[source, rows],
-            dst_ref=gath.at[source, rows],
-            send_sem=gsend.at[p, slot],
-            recv_sem=grecv.at[p, slot],
-            device_id=(me + delta[g_orders[p][s]],),
-            device_id_type=MESH,
+            src_ref=src, dst_ref=dst, send_sem=send, recv_sem=recv_at,
+            device_id=(to,), device_id_type=MESH,
         )
 
-    def gather_start(p, s, wave):
-        def body(k):
-            source = me + spread(k, g_orders[p][:s])
-
-            @pl.when(in_wave(source, wave))
-            def _():
-                gather_copy(p, s, k, source, s == 0).start()
-
-        each(1 << s, body)
-
-    def gather_sent(p, s, wave):
-        def body(k):
-            source = me + spread(k, g_orders[p][:s])
-
-            @pl.when(in_wave(source, wave))
-            def _():
-                gather_copy(p, s, k, source, s == 0).wait_send()
-
-        each(1 << s, body)
-
-    def gather_arrive(p, s, wave):
-        def body(k):
-            source = me + delta[g_orders[p][s]] + spread(k, g_orders[p][:s])
-
-            @pl.when(in_wave(source, wave))
-            def _():
-                gather_copy(p, s, k, source, False).wait_recv()
-
-        each(1 << s, body)
-
-    def gather_round(s, wave):
+    def gather_upper(p, j):
+        return remote(
+            mine_ref.at[pl.ds(p * part, part)], gath.at[p, spots[p], up],
+            gu_send.at[p, j - 1], gu_recv.at[p, j - 1], peer(j),
+        )
+
+    def gather_low(p, i, wave):
+        held = gath.at[p, pl.ds(fixed(p, i), 1 << i), waves[wave]]
+        return remote(
+            held, held, gl_send.at[wave, p, i], gl_recv.at[wave, p, i],
+            me + delta[orders[p][i]],
+        )
+
+    def send_own():
         for p in range(PARTS):
-            gather_arrive(p, s, wave)
-            if s + 1 < bits:
-                gather_start(p, s + 1, wave)
-
-    def reduce_copy(p, s, k, block):
-        slot = n - (n >> s) + k
-        return pltpu.make_async_remote_copy(
-            src_ref=gath.at[block, pl.ds(p * part, part)],
-            dst_ref=recv.at[p, slot],
-            send_sem=rsend.at[p, slot],
-            recv_sem=rrecv.at[p, slot],
-            device_id=(me + delta[r_orders[p][s]],),
-            device_id_type=MESH,
+            for j in range(1, uppers):
+                gather_upper(p, j).start()
+
+    def gather_upper_arrive(p, wave):
+        own = gath.at[p, spots[p], up]
+        if wave == 0:
+            @pl.when(up > 0)
+            def _():
+                remote(own, own, gu_send.at[p, 0], gu_recv.at[p, up - 1], me).wait_recv()
+        else:
+            for j in range(1, uppers):
+                @pl.when(up != j)
+                def _():
+                    remote(own, own, gu_send.at[p, 0], gu_recv.at[p, j - 1], me).wait_recv()
+        gather_low(p, 0, wave).start()
+
+    def gather_round(i, wave):
+        for p in range(PARTS):
+            gather_low(p, i, wave).wait_recv()
+            if i + 1 < e:
+                gather_low(p, i + 1, wave).start()
+
+    def zero_from(i):
+        return sum(bit[b] for b in orders[0][i:]) if i < e else 0
+
+    def head_gather_upper(wait):
+        if wait:
+            @pl.when(zero_from(0) + (up == 1).astype(jnp.int32) == 0)
+            def _():
+                at = up + 1 - 2 * (up % 2) - 1
+                remote(head_v, head_v, gh_send.at[0], gh_recv.at[at], me).wait_recv()
+        else:
+            @pl.when(me == near_count)
+            def _():
+                head_v[...] = mine_ref[0:16, :]
+                for j in range(1, uppers):
+                    remote(
+                        mine_ref.at[0:16], head_v, gh_send.at[j - 1], gh_recv.at[j - 1], peer(j)
+                    ).start()
+
+    def head_gather_low(i, wait):
+        at = uppers - 1 + i
+        copy = remote(head_v, head_v, gh_send.at[at], gh_recv.at[at], me + delta[orders[0][i]])
+        if wait:
+            @pl.when(zero_from(i + 1) * 2 + bit[orders[0][i]] == 1)
+            def _():
+                copy.wait_recv()
+        else:
+            @pl.when(zero_from(i) == 0)
+            def _():
+                copy.start()
+
+    def gather_sent():
+        for p in range(PARTS):
+            for j in range(1, uppers):
+                gather_upper(p, j).wait_send()
+            for i in range(e):
+                for wave in range(2):
+                    gather_low(p, i, wave).wait_send()
+        if head:
+            @pl.when(me == near_count)
+            def _():
+                for j in range(1, uppers):
+                    remote(
+                        mine_ref.at[0:16], head_v, gh_send.at[j - 1], gh_recv.at[j - 1], peer(j)
+                    ).wait_send()
+            for i in range(e):
+                @pl.when(zero_from(i) == 0)
+                def _():
+                    at = uppers - 1 + i
+                    remote(
+                        head_v, head_v, gh_send.at[at], gh_recv.at[at], me + delta[orders[0][i]]
+                    ).wait_send()
+
+    def reduce_low(p, i, wave):
+        other = fixed(p, i + 1) + (1 - bit[orders[p][i]]) * (1 << i)
+        return remote(
+            gath.at[p, pl.ds(other, 1 << i), waves[wave]],
+            recv.at[p, pl.ds((1 << i) - 1, 1 << i), waves[wave]],
+            rl_send.at[wave, p, i], rl_recv.at[wave, p, i], me + delta[orders[p][i]],
         )
 
-    def reduce_start(p, s, wave):
-        order = r_orders[p]
-
-        def body(k):
-            block = me + delta[order[s]] + spread(k, order[s + 1 :])
-
-            @pl.when(in_wave(block, wave))
-            def _():
-                reduce_copy(p, s, k, block).start()
-
-        each(n >> (s + 1), body)
-
-    def reduce_sent(p, s, wave):
-        order = r_orders[p]
-
-        def body(k):
-            block = me + delta[order[s]] + spread(k, order[s + 1 :])
-
-            @pl.when(in_wave(block, wave))
-            def _():
-                reduce_copy(p, s, k, block).wait_send()
-
-        each(n >> (s + 1), body)
-
-    def reduce_absorb(p, s, wave):
-        rows = pl.ds(p * part, part)
-
-        def body(k):
-            block = me + spread(k, r_orders[p][s + 1 :])
-
-            @pl.when(in_wave(block, wave))
-            def _():
-                reduce_copy(p, s, k, block).wait_recv()
-                slot = n - (n >> s) + k
-                total = gath[block, rows].astype(F32) + recv[p, slot].astype(F32)
-                if s + 1 == bits:
-                    flat_ref[rows, :] = total
-                else:
-                    gath[block, rows] = total.astype(BF)
-
-        each(n >> (s + 1), body)
-
-    def reduce_round(s, wave):
+    def reduce_upper(p, j, block, to):
+        return remote(
+            gath.at[p, spots[p], block], recv_up.at[p, j - 1],
+            ru_send.at[p, j - 1], ru_recv.at[p, j - 1], to,
+        )
+
+    def reduce_upper_start(p, wave):
+        if wave == 0:
+            @pl.when(up > 0)
+            def _():
+                reduce_upper(p, up, 0, near_me).start()
+        else:
+            for j in range(1, uppers):
+                @pl.when(up != j)
+                def _():
+                    reduce_upper(p, j, peer(j) // near_count, peer(j)).start()
+
+    def reduce_round(i, wave):
         for p in range(PARTS):
-            reduce_absorb(p, s, wave)
-            if s + 1 < bits:
-                reduce_start(p, s + 1, wave)
+            reduce_low(p, i, wave).wait_recv()
+            keep = pl.ds(fixed(p, i), 1 << i)
+            slot = pl.ds((1 << i) - 1, 1 << i)
+            total = gath[p, keep, waves[wave]].astype(F32) + recv[p, slot, waves[wave]].astype(F32)
+            gath[p, keep, waves[wave]] = total.astype(BF)
+            if i > 0:
+                reduce_low(p, i - 1, wave).start()
+            else:
+                reduce_upper_start(p, wave)
+
+    def reduce_last(wave):
+        @pl.when(up == 0 if wave == 0 else up > 0)
+        def _():
+            for p in range(PARTS):
+                total = gath[p, spots[p], up].astype(F32)
+                for j in range(1, uppers):
+                    reduce_upper(p, j, 0, me).wait_recv()
+                    total = total + recv_up[p, j - 1].astype(F32)
+                flat_ref[p * part : (p + 1) * part, :] = total
+
+    def head_reduce_low(i):
+        copy = remote(
+            head_v, head_in.at[i], rh_send.at[0], rh_recv.at[i], me + delta[orders[0][i]]
+        )
+
+        @pl.when(zero_from(i + 1) * 2 + bit[orders[0][i]] == 1)
+        def _():
+            copy.start()
+            copy.wait_send()
+
+        @pl.when(zero_from(i) == 0)
+        def _():
+            copy.wait_recv()
+            head_v[...] = (head_v[...].astype(F32) + head_in[i].astype(F32)).astype(BF)
+
+    def head_reduce_upper():
+        @pl.when(zero_from(0) + (up == 1).astype(jnp.int32) == 0)
+        def _():
+            at = up + 1 - 2 * (up % 2) - 1
+            copy = remote(head_v, head_in.at[e + at], rh_send.at[0], rh_recv.at[e + at], near_count)
+            copy.start()
+            copy.wait_send()
+
+        @pl.when(me == near_count)
+        def _():
+            total = head_v[...].astype(F32)
+            for j in range(1, uppers):
+                at = e + j - 1
+                remote(head_v, head_in.at[at], rh_send.at[0], rh_recv.at[at], me).wait_recv()
+                total = total + head_in[at].astype(F32)
+            flat_ref[0:16, :] = total
+
+    def reduce_sent():
+        for p in range(PARTS):
+            for j in range(1, uppers):
+                reduce_upper(p, j, 0, me).wait_send()
+            for i in range(e):
+                for wave in range(2):
+                    reduce_low(p, i, wave).wait_send()
+
+    def home(d, p):
+        return p, place(d % near_count, orders[p]), d // near_count
 
     def unpack(blocks):
         for d in blocks:
             first, shift = divmod(shard * d, LANES)
             rows = (shift + shard + LANES - 1) // LANES
-            piece = gath[d].astype(F32)
-            if d > 0 and shift:
-                seam = buf[first : first + 1, :] + piece[0:1]
-                buf[first : first + rows, :] = piece[:rows]
-                buf[first : first + 1, :] = seam
-            else:
-                buf[first : first + rows, :] = piece[:rows]
+            for p in range(PARTS):
+                count = min(part, rows - p * part)
+                if count <= 0:
+                    break
+                at = first + p * part
+                piece = gath[home(d, p)].astype(F32)
+                if d > 0 and shift and p == 0:
+                    seam = buf[at : at + 1, :] + piece[0:1]
+                    buf[at : at + count, :] = piece[:count]
+                    buf[at : at + 1, :] = seam
+                else:
+                    buf[at : at + count, :] = piece[:count]
+
+    def unpack_head():
+        first, shift = divmod(shard * near_count, LANES)
+        piece = head_v[...].astype(F32)
+        if shift:
+            piece = piece + jnp.where(
+                lax.broadcasted_iota(jnp.int32, piece.shape, 0) == 0, buf[first : first + 16, :], 0.0
+            )
+        buf[first : first + 16, :] = piece
 
     def load_matrix(k, rows, blocks, start):
         for b in range(blocks):
@@ -262,7 +361,9 @@
     def pack(blocks):
         for d in blocks:
             first = shard * d // LANES
-            gath[d] = buf[first : first + window, :].astype(BF)
+            for p in range(PARTS):
+                at = first + p * part
+                gath[home(d, p)] = buf[at : at + part, :].astype(BF)
 
     def param(i):
         return vec[i : i + 1, :]
@@ -273,14 +374,20 @@
     ]
     for c in loads:
         c.start()
+    partners = [me + delta[b] for b in range(e)] + [peer(j) for j in range(1, uppers)]
     barrier = pltpu.get_barrier_semaphore()
-    for b in range(bits):
-        pl.semaphore_signal(barrier, inc=1, device_id=(me + delta[b],), device_id_type=MESH)
-    pl.semaphore_wait(barrier, bits)
-    for wave in range(2):
-        for p in range(PARTS):
-            gather_start(p, 0, wave)
-    gath[me] = mine_ref[...]
+    for partner in partners:
+        pl.semaphore_signal(barrier, inc=1, device_id=(partner,), device_id_type=MESH)
+    pl.semaphore_wait(barrier, len(partners))
+
+    @pl.when(up == 0)
+    def _():
+        send_own()
+
+    if head:
+        head_gather_upper(False)
+    for p in range(PARTS):
+        gath[p, spots[p], up] = mine_ref[p * part : (p + 1) * part, :]
 
     def scatter_rows(source, target, scales):
         for c in range(3):
@@ -298,12 +405,28 @@
     masks = [(g < live).astype(F32) for g in range(slots)]
     loads[0].wait()
     scatter_rows(img_v, x_s, None)
-    gather_round(0, 0)
+    for p in range(PARTS):
+        gather_upper_arrive(p, 0)
+
+    @pl.when(up > 0)
+    def _():
+        send_own()
+
+    if head:
+        head_gather_upper(True)
     loads[1].wait()
+    if head:
+        head_gather_low(0, False)
     scatter_rows(cot_v, dout_s, masks)
-    for s in range(1, bits):
-        gather_round(s, 0)
-    unpack(range(early))
+    for i in range(e):
+        gather_round(i, 0)
+        if head:
+            head_gather_low(i, True)
+            if i + 1 < e:
+                head_gather_low(i + 1, False)
+    unpack(range(near_count))
+    if head:
+        unpack_head()
     load_matrix(*matrices()[0])
     load_vectors((G1, S1, BQ, BV))
     gvec[...] = jnp.zeros_like(gvec)
@@ -352,21 +475,22 @@
     trips = tiles // UNROLL
 
     def forward(i, carry):
-        for s in range(bits):
-            @pl.when(i == (s * trips) // bits)
-            def _():
-                gather_round(s, 1)
+        for r in range(e + 1):
+            @pl.when(i == (r * trips) // (e + 1))
+            def _():
+                if r == 0:
+                    for p in range(PARTS):
+                        gather_upper_arrive(p, 1)
+                else:
+                    gather_round(r - 1, 1)
 
         for u in range(UNROLL):
             attend(i * UNROLL + u)
         return carry
 
     lax.fori_loop(0, trips, forward, 0)
-    for wave in range(2):
-        for p in range(PARTS):
-            for s in range(bits):
-                gather_sent(p, s, wave)
-    unpack(range(early, n))
+    gather_sent()
+    unpack(range(near_count, n))
     for m in matrices()[1:]:
         load_matrix(*m)
     load_vectors((BO, G2, S2, BD))
@@ -453,9 +577,9 @@
         buf[pl.ds(3 * ROW_OUT + b, D, 3), :] = grad[:, b * LANES : (b + 1) * LANES]
     for i in (BO, G2, S2, BD):
         put_vector(i, gvec[i : i + 1, :])
-    pack(range(early, n))
+    pack(range(near_count, n))
     for p in range(PARTS):
-        reduce_start(p, 0, 1)
+        reduce_low(p, e - 1, 1).start()
     gather_back(masks, res_s)
     emit_rows(img_v)
     out_copy = pltpu.make_async_copy(img_v, out_ref, load_sem.at[2])
@@ -481,10 +605,13 @@
         qkv_s[rows, cv] = dvalue.astype(BF)
 
     def backward(i, carry):
-        for s in range(bits):
-            @pl.when(i == ((s + 1) * trips) // (bits + 1))
-            def _():
-                reduce_round(s, 1)
+        for r in range(e + 1):
+            @pl.when(i == ((r + 1) * trips) // (e + 2))
+            def _():
+                if r < e:
+                    reduce_round(e - 1 - r, 1)
+                else:
+                    reduce_last(1)
 
         for u in range(UNROLL):
             attend_back(i * UNROLL + u)
@@ -514,19 +641,24 @@
     lax.fori_loop(0, 3, grad_qkv, 0)
     for i in (G1, S1, BQ, BV):
         put_vector(i, gvec[i : i + 1, :])
-    pack(range(early))
+    pack(range(near_count))
     for p in range(PARTS):
-        reduce_start(p, 0, 0)
+        reduce_low(p, e - 1, 0).start()
+    if head:
+        at = shard * near_count // LANES
+        head_v[...] = buf[at : at + 16, :].astype(BF)
     gather_back(None, res_s)
     emit_rows(cot_v)
     din_copy = pltpu.make_async_copy(cot_v, din_ref, load_sem.at[3])
     din_copy.start()
-    for s in range(bits):
-        reduce_round(s, 0)
-    for wave in range(2):
-        for p in range(PARTS):
-            for s in range(bits):
-                reduce_sent(p, s, wave)
+    for i in reversed(range(e)):
+        reduce_round(i, 0)
+        if head:
+            head_reduce_low(i)
+    if head:
+        head_reduce_upper()
+    reduce_last(0)
+    reduce_sent()
     out_copy.wait()
     din_copy.wait()
 
@@ -540,7 +672,13 @@
     whole = pl.BlockSpec(memory_space=pltpu.VMEM)
     apart = pl.BlockSpec(memory_space=pl.ANY)
     VM = pltpu.VMEM
-    sems = pltpu.SemaphoreType.DMA((PARTS, n - 1))
+    e, _ = plan(n, shard)
+    near_count, uppers = 1 << e, n >> e
+    part = window // PARTS
+    DMA = pltpu.SemaphoreType.DMA
+    across = DMA((PARTS, uppers - 1))
+    inside = DMA((2, PARTS, e))
+    tops = DMA((uppers - 1 + e,))
     out, din, mine = pl.pallas_call(
         functools.partial(step_kernel, n, shard, slots, tok, tokp),
         in_specs=[pl.BlockSpec(memory_space=pltpu.SMEM), whole, apart, apart],
@@ -551,8 +689,10 @@
             jax.ShapeDtypeStruct((window, LANES), F32),
         ],
         scratch_shapes=[
-            VM((n, window, LANES), BF),
-            VM((PARTS, n - 1, window // PARTS, LANES), BF),
+            VM((PARTS, near_count, uppers, part, LANES), BF),
+            VM((PARTS, near_count - 1, uppers, part, LANES), BF),
+            VM((PARTS, uppers - 1, part, LANES), BF),
+            VM((16, LANES), BF), VM((e + uppers - 1, 16, LANES), BF),
             VM((buf_rows, LANES), F32),
             VM((D, 3 * D), BF), VM((D, D), BF), VM((D, FF), BF), VM((FF, D), BF),
             VM((8, D), F32), VM((1, FF), F32), VM((8, D), F32),
@@ -561,7 +701,8 @@
             VM((rows, 3 * D), BF), VM((slots * PAIRS, 2 * tokp, tokp), BF),
             VM((rows, D), BF),
             VM((rows, D), F32), VM((rows, 1), F32), VM((rows, D), F32), VM((rows, D), F32), VM((rows, D), BF),
-            pltpu.SemaphoreType.DMA((4,)), sems, sems, sems, sems,
+            DMA((4,)), across, across, inside, inside, across, across, inside, inside,
+            tops, tops, DMA((1,)), tops,
         ],
         compiler_params=pltpu.CompilerParams(
             collective_id=1, has_side_effects=True, vmem_limit_bytes=67043328

time: 159 us -> 136 us (0.86)
  Pallas kernels: 150 us -> 127 us
    pallas_call x1, Pallas kernels: 150 us -> 127 us  [run_step(): pl.pallas_call(functools.partial(step_kernel, n, shard, slots, tok, tokp)...]
where the time goes in v2:
time: 136 us; the launch traced here: 135 us
  Pallas kernels  127 us (93%)
  local copies, waits for them, and re-layouts  6.26 us (5%)
    pallas_call x1, Pallas kernels, run_step(): pl.pallas_call(functools.partial(step_kernel, n, shard, slots, tok, tokp)...  127 us
    unnamed x4, local copies, waits for them, and re-layouts  3.55 us

profile of v2, /device:TPU:0, one launch (start us, length us, event | category | flops | bytes accessed | tf_op | source)
XLA Modules:
  0.0 135.4 jit_solution(2914459660281575998)
XLA Ops:
  1.3 1.0 pad.4
  2.3 1.2 fusion.2.mine_ref
  3.4 126.7 %step.1 = (bf16[1576,384]{1,0:T(8,128)(2,1)}, bf16[1576,384]{1,0:T(8,128)(2,1)}, f32[448,128]{1,0:T(8,128)}) custom-call(s32[1]{0:T(128)S(6)} %copy.9.live_ref, bf16[448,128]{1,0:T(8,128)(2,1)} %fusion.2.mine_ref, bf16[1576,384]{1,0:T(8,128)(2,1)} %bitcast.17, bf16[1576,384]{1,0:T(8,128)(2,1)} %bitcast.18), custom_call_target="tpu_custom_call" | custom-call | tf_op jit(solution)/shard_map/step/pallas_call | solution.py:682
  130.1 1.8 %dynamic_slice.8 = f32[55440]{0:T(1024)} dynamic-slice(f32[57344]{0:T(1024)} %bitcast.19, s32[]{:T(128)S(6)} %select_n.25), dynamic_slice_sizes={55440} | dynamic-slice | bytes 443524 | tf_op jit(solution)/shard_map/dynamic_slice | solution.py:727
  131.9 0.0 copy-start
  131.9 2.5 %copy.10 = bf16[8,197,384]{2,0,1:T(8,128)(2,1)} copy(bf16[8,197,384]{2,0,1:T(8,128)(2,1)} %bitcast.16) | data formatting | bytes 2420736
  134.4 0.0 copy-done
  134.4 1.0 copy.11
Async XLA Ops:
  131.9 2.5 %copy-start = (bf16[1576,384]{1,0:T(8,128)(2,1)S(1)}, bf16[1576,384]{1,0:T(8,128)(2,1)}, u32[]{:S(2)}) copy-start(bf16[1576,384]{1,0:T(8,128)(2,1)} %get-tuple-element.7) | copy-start | bytes 3631108

commit v3 on v2

--- a/solution.py
+++ b/solution.py
@@ -27,9 +27,9 @@
 VEC_ROWS = (0, 1, ROW_OUT - 2, ROW_OUT - 1, ROW_UP - 3, ROW_UP - 2, ROW_UP - 1, ROW_BDOWN)
 G1, S1, BQ, BV, BO, G2, S2, BD = range(8)
 
-CHUNK = 256
+CHUNK = 512
 PARTS = 4
-UNROLL = 2
+UNROLL = 4
 BLOCKS = 4
 MESH = pl.DeviceIdType.MESH
 
@@ -460,16 +460,16 @@
     def stack(v, scale=1.0):
         return jnp.concatenate([v * (low_b * scale), v * (high_b * scale)], axis=0)
 
-    def attend(t):
-        rows, (cq, ck, cv) = views(t)
-        q, k, v = qkv_s[rows, cq], qkv_s[rows, ck], qkv_s[rows, cv]
-        s = nt(stack(q, HD**-0.5), k)
-        s = jnp.where(key_ok, s, -1e30)
-        e = jnp.exp(s - jnp.max(s, axis=-1, keepdims=True))
-        probs = (e * (1.0 / jnp.sum(e, axis=-1, keepdims=True))).astype(BF)
-        probs_s[t] = probs
-        mixed = nn(probs, v)
-        mixed_s[rows, cq] = jnp.where(low, mixed[:tokp], mixed[tokp:]).astype(BF)
+    def attend(tiles_now):
+        at = [views(t) for t in tiles_now]
+        q, k, v = ([qkv_s[rows, c[j]] for rows, c in at] for j in range(3))
+        s = [jnp.where(key_ok, nt(stack(a, HD**-0.5), b), -1e30) for a, b in zip(q, k)]
+        e = [jnp.exp(a - jnp.max(a, axis=-1, keepdims=True)) for a in s]
+        probs = [(a * (1.0 / jnp.sum(a, axis=-1, keepdims=True))).astype(BF) for a in e]
+        mixed = [nn(a, b) for a, b in zip(probs, v)]
+        for t, (rows, c), a, m in zip(tiles_now, at, probs, mixed):
+            probs_s[t] = a
+            mixed_s[rows, c[0]] = jnp.where(low, m[:tokp], m[tokp:]).astype(BF)
 
     tiles = slots * PAIRS
     trips = tiles // UNROLL
@@ -484,8 +484,7 @@
                 else:
                     gather_round(r - 1, 1)
 
-        for u in range(UNROLL):
-            attend(i * UNROLL + u)
+        attend([i * UNROLL + u for u in range(UNROLL)])
         return carry
 
     lax.fori_loop(0, trips, forward, 0)
@@ -585,24 +584,25 @@
     out_copy = pltpu.make_async_copy(img_v, out_ref, load_sem.at[2])
     out_copy.start()
 
-    def attend_back(t):
-        rows, (cq, ck, cv) = views(t)
-        q, k, v = qkv_s[rows, cq], qkv_s[rows, ck], qkv_s[rows, cv]
-        dm = stack(ffn_s[rows, cq])
-        probs = probs_s[t]
-        wide = probs.astype(F32)
-        dprobs = nt(dm, v)
-        delta_p = jnp.sum(wide * dprobs, axis=-1, keepdims=True)
-        ds = (wide * (dprobs - delta_p)).astype(BF)
-        dvalue = tn(probs, dm)
-        dq = nn(ds, k)
-        dquery = jnp.where(low, dq[:tokp], dq[tokp:]) * (HD**-0.5)
-        dkey = tn(ds, stack(q, HD**-0.5))
-        gvec[BQ : BQ + 1, cq] += colsum(dquery)
-        gvec[BV : BV + 1, cq] += colsum(dvalue)
-        qkv_s[rows, cq] = dquery.astype(BF)
-        qkv_s[rows, ck] = dkey.astype(BF)
-        qkv_s[rows, cv] = dvalue.astype(BF)
+    def attend_back(tiles_now):
+        at = [views(t) for t in tiles_now]
+        q, k, v = ([qkv_s[rows, c[j]] for rows, c in at] for j in range(3))
+        dm = [stack(ffn_s[rows, c[0]]) for rows, c in at]
+        probs = [probs_s[t] for t in tiles_now]
+        dprobs = [nt(a, b) for a, b in zip(dm, v)]
+        dvalue = [tn(a, b) for a, b in zip(probs, dm)]
+        wide = [a.astype(F32) for a in probs]
+        delta_p = [jnp.sum(a * b, axis=-1, keepdims=True) for a, b in zip(wide, dprobs)]
+        ds = [(a * (b - c)).astype(BF) for a, b, c in zip(wide, dprobs, delta_p)]
+        dq = [nn(a, b) for a, b in zip(ds, k)]
+        dkey = [tn(a, stack(b, HD**-0.5)) for a, b in zip(ds, q)]
+        dquery = [jnp.where(low, a[:tokp], a[tokp:]) * (HD**-0.5) for a in dq]
+        for (rows, (cq, ck, cv)), a, b, c in zip(at, dquery, dkey, dvalue):
+            gvec[BQ : BQ + 1, cq] += colsum(a)
+            gvec[BV : BV + 1, cq] += colsum(c)
+            qkv_s[rows, cq] = a.astype(BF)
+            qkv_s[rows, ck] = b.astype(BF)
+            qkv_s[rows, cv] = c.astype(BF)
 
     def backward(i, carry):
         for r in range(e + 1):
@@ -613,8 +613,7 @@
                 else:
                     reduce_last(1)
 
-        for u in range(UNROLL):
-            attend_back(i * UNROLL + u)
+        attend_back([i * UNROLL + u for u in range(UNROLL)])
         return carry
 
     lax.fori_loop(0, trips, backward, 0)

time: 136 us -> 127 us (0.934)
  Pallas kernels: 127 us -> 118 us
    pallas_call x1, Pallas kernels: 127 us -> 118 us  [run_step(): pl.pallas_call(functools.partial(step_kernel, n, shard, slots, tok, tokp)...]
where the time goes in v3:
time: 127 us
  Pallas kernels  118 us (93%)
  local copies, waits for them, and re-layouts  6.26 us (5%)
  between operations  1.33 us (1%)
    pallas_call x1, Pallas kernels, run_step(): pl.pallas_call(functools.partial(step_kernel, n, shard, slots, tok, tokp)...  118 us
    unnamed x4, local copies, waits for them, and re-layouts  3.55 us

profile of v3, /device:TPU:0, one launch (start us, length us, event | category | flops | bytes accessed | tf_op | source)
XLA Modules:
  0.0 126.7 jit_solution(16746081939000981582)
XLA Ops:
  1.3 1.0 pad.4
  2.3 1.2 fusion.2.mine_ref
  3.4 117.9 %step.1 = (bf16[1576,384]{1,0:T(8,128)(2,1)}, bf16[1576,384]{1,0:T(8,128)(2,1)}, f32[448,128]{1,0:T(8,128)}) custom-call(s32[1]{0:T(128)S(6)} %copy.9.live_ref, bf16[448,128]{1,0:T(8,128)(2,1)} %fusion.2.mine_ref, bf16[1576,384]{1,0:T(8,128)(2,1)} %bitcast.17, bf16[1576,384]{1,0:T(8,128)(2,1)} %bitcast.18), custom_call_target="tpu_custom_call" | custom-call | tf_op jit(solution)/shard_map/step/pallas_call | solution.py:681
  121.4 1.8 %dynamic_slice.8 = f32[55440]{0:T(1024)} dynamic-slice(f32[57344]{0:T(1024)} %bitcast.19, s32[]{:T(128)S(6)} %select_n.25), dynamic_slice_sizes={55440} | dynamic-slice | bytes 443524 | tf_op jit(solution)/shard_map/dynamic_slice | solution.py:726
  123.1 0.0 copy-start
  123.1 2.5 %copy.10 = bf16[8,197,384]{2,0,1:T(8,128)(2,1)} copy(bf16[8,197,384]{2,0,1:T(8,128)(2,1)} %bitcast.16) | data formatting | bytes 2420736
  125.7 0.0 copy-done
  125.7 1.0 copy.11
Async XLA Ops:
  123.1 2.5 %copy-start = (bf16[1576,384]{1,0:T(8,128)(2,1)S(1)}, bf16[1576,384]{1,0:T(8,128)(2,1)}, u32[]{:S(2)}) copy-start(bf16[1576,384]{1,0:T(8,128)(2,1)} %get-tuple-element.7) | copy-start | bytes 3631108

commit v4 on v3

--- a/solution.py
+++ b/solution.py
@@ -32,6 +32,7 @@
 UNROLL = 4
 BLOCKS = 4
 MESH = pl.DeviceIdType.MESH
+HALVES = (range(0, PARTS // 2), range(PARTS // 2, PARTS))
 
 
 def up_to(value, unit):
@@ -77,6 +78,10 @@
 
 def place(low, order):
     return sum((low >> b & 1) << i for i, b in enumerate(order))
+
+
+def reduce_waves(uppers):
+    return [(0, 1), (1, 2)] + ([(2, uppers)] if uppers > 2 else [])
 
 
 def plan(n, shard):
@@ -123,6 +128,7 @@
     orders = low_orders(e)
     spots = [sum(bit[b] * (1 << i) for i, b in enumerate(order)) for order in orders]
     waves = (pl.ds(0, 1), pl.ds(1, uppers - 1))
+    r_waves = reduce_waves(uppers)
 
     def peer(j):
         return me + sum(delta[e + b] for b in range(bits - e) if j >> b & 1)
@@ -167,8 +173,8 @@
                     remote(own, own, gu_send.at[p, 0], gu_recv.at[p, j - 1], me).wait_recv()
         gather_low(p, 0, wave).start()
 
-    def gather_round(i, wave):
-        for p in range(PARTS):
+    def gather_round(i, wave, parts=range(PARTS)):
+        for p in parts:
             gather_low(p, i, wave).wait_recv()
             if i + 1 < e:
                 gather_low(p, i + 1, wave).start()
@@ -225,11 +231,15 @@
                         head_v, head_v, gh_send.at[at], gh_recv.at[at], me + delta[orders[0][i]]
                     ).wait_send()
 
+    def span(wave):
+        first, last = r_waves[wave]
+        return pl.ds(first, last - first)
+
     def reduce_low(p, i, wave):
         other = fixed(p, i + 1) + (1 - bit[orders[p][i]]) * (1 << i)
         return remote(
-            gath.at[p, pl.ds(other, 1 << i), waves[wave]],
-            recv.at[p, pl.ds((1 << i) - 1, 1 << i), waves[wave]],
+            gath.at[p, pl.ds(other, 1 << i), span(wave)],
+            recv.at[p, pl.ds((1 << i) - 1, 1 << i), span(wave)],
             rl_send.at[wave, p, i], rl_recv.at[wave, p, i], me + delta[orders[p][i]],
         )
 
@@ -240,23 +250,21 @@
         )
 
     def reduce_upper_start(p, wave):
-        if wave == 0:
-            @pl.when(up > 0)
-            def _():
-                reduce_upper(p, up, 0, near_me).start()
-        else:
-            for j in range(1, uppers):
-                @pl.when(up != j)
-                def _():
-                    reduce_upper(p, j, peer(j) // near_count, peer(j)).start()
+        first, last = r_waves[wave]
+        for j in range(1, uppers):
+            to = peer(j) // near_count
+
+            @pl.when((to >= first) & (to < last))
+            def _():
+                reduce_upper(p, j, to, peer(j)).start()
 
     def reduce_round(i, wave):
         for p in range(PARTS):
             reduce_low(p, i, wave).wait_recv()
             keep = pl.ds(fixed(p, i), 1 << i)
             slot = pl.ds((1 << i) - 1, 1 << i)
-            total = gath[p, keep, waves[wave]].astype(F32) + recv[p, slot, waves[wave]].astype(F32)
-            gath[p, keep, waves[wave]] = total.astype(BF)
+            total = gath[p, keep, span(wave)].astype(F32) + recv[p, slot, span(wave)].astype(F32)
+            gath[p, keep, span(wave)] = total.astype(BF)
             if i > 0:
                 reduce_low(p, i - 1, wave).start()
             else:
@@ -295,6 +303,7 @@
             copy.start()
             copy.wait_send()
 
+    def head_reduce_last():
         @pl.when(me == near_count)
         def _():
             total = head_v[...].astype(F32)
@@ -309,7 +318,7 @@
             for j in range(1, uppers):
                 reduce_upper(p, j, 0, me).wait_send()
             for i in range(e):
-                for wave in range(2):
+                for wave in range(len(r_waves)):
                     reduce_low(p, i, wave).wait_send()
 
     def home(d, p):
@@ -424,6 +433,8 @@
             head_gather_low(i, True)
             if i + 1 < e:
                 head_gather_low(i + 1, False)
+    for p in range(PARTS):
+        gather_upper_arrive(p, 1)
     unpack(range(near_count))
     if head:
         unpack_head()
@@ -438,6 +449,11 @@
         return pl.ds(pl.multiple_of(i * height, 16), height)
 
     def project(i, carry):
+        for half in range(2):
+            @pl.when(i == 1 + half * (BLOCKS - 2))
+            def _():
+                gather_round(0, 1, HALVES[half])
+
         hat1, _ = norm_stats(x_s[band(i), :].astype(F32))
         attn_in = (hat1 * param(G1) + param(S1)).astype(BF)
         attn_s[band(i), :] = attn_in
@@ -475,19 +491,17 @@
     trips = tiles // UNROLL
 
     def forward(i, carry):
-        for r in range(e + 1):
-            @pl.when(i == (r * trips) // (e + 1))
-            def _():
-                if r == 0:
-                    for p in range(PARTS):
-                        gather_upper_arrive(p, 1)
-                else:
-                    gather_round(r - 1, 1)
+        for r in range(1, e - 1):
+            for half in range(2):
+                @pl.when(i == (trips * (2 * r + half) - 1) // (2 * e - 3))
+                def _():
+                    gather_round(r, 1, HALVES[half])
 
         attend([i * UNROLL + u for u in range(UNROLL)])
         return carry
 
     lax.fori_loop(0, trips, forward, 0)
+    gather_round(e - 1, 1)
     gather_sent()
     unpack(range(near_count, n))
     for m in matrices()[1:]:
@@ -514,6 +528,7 @@
         return carry
 
     lax.fori_loop(0, BLOCKS, second_norm, 0)
+    put_vector(BD, gvec[BD : BD + 1, :])
 
     def feed(c, carry):
         cols = pl.ds(pl.multiple_of(c * CHUNK, CHUNK), CHUNK)
@@ -542,6 +557,16 @@
         return carry
 
     lax.fori_loop(0, FF // CHUNK, feed, 0)
+    assert shard * 2 * near_count // LANES >= 3 * ROW_UP
+
+    def send_blocks(wave):
+        first, last = r_waves[wave]
+        pack(range(first * near_count, last * near_count))
+        for p in range(PARTS):
+            reduce_low(p, e - 1, wave).start()
+
+    for wave in range(2, len(r_waves)):
+        send_blocks(wave)
 
     def gather_back(value, source_ref):
         for g in range(slots):
@@ -574,11 +599,9 @@
     grad = tn(mixed_s[...], dout_s[...])
     for b in range(3):
         buf[pl.ds(3 * ROW_OUT + b, D, 3), :] = grad[:, b * LANES : (b + 1) * LANES]
-    for i in (BO, G2, S2, BD):
+    for i in (BO, G2, S2):
         put_vector(i, gvec[i : i + 1, :])
-    pack(range(near_count, n))
-    for p in range(PARTS):
-        reduce_low(p, e - 1, 1).start()
+    send_blocks(1)
     gather_back(masks, res_s)
     emit_rows(img_v)
     out_copy = pltpu.make_async_copy(img_v, out_ref, load_sem.at[2])
@@ -605,13 +628,12 @@
             qkv_s[rows, cv] = c.astype(BF)
 
     def backward(i, carry):
-        for r in range(e + 1):
-            @pl.when(i == ((r + 1) * trips) // (e + 2))
-            def _():
-                if r < e:
-                    reduce_round(e - 1 - r, 1)
-                else:
-                    reduce_last(1)
+        late = list(range(len(r_waves) - 1, 0, -1))
+        points = (e - 1) * len(late)
+        for k in range(points):
+            @pl.when(i == 1 + (k * (trips - 1)) // points)
+            def _():
+                reduce_round(e - 1 - k // len(late), late[k % len(late)])
 
         attend_back([i * UNROLL + u for u in range(UNROLL)])
         return carry
@@ -619,6 +641,11 @@
     lax.fori_loop(0, trips, backward, 0)
 
     def first_norm_back(i, carry):
+        for k in range(1, len(r_waves)):
+            @pl.when(i == 2 * (len(r_waves) - k) - 1)
+            def _():
+                reduce_round(0, k)
+
         rows = band(i)
         dn1 = nt(qkv_s[rows, :], wqkv[...])
         hat1, inv1 = norm_stats(x_s[rows, :].astype(F32))
@@ -640,9 +667,7 @@
     lax.fori_loop(0, 3, grad_qkv, 0)
     for i in (G1, S1, BQ, BV):
         put_vector(i, gvec[i : i + 1, :])
-    pack(range(near_count))
-    for p in range(PARTS):
-        reduce_low(p, e - 1, 0).start()
+    send_blocks(0)
     if head:
         at = shard * near_count // LANES
         head_v[...] = buf[at : at + 16, :].astype(BF)
@@ -656,7 +681,10 @@
             head_reduce_low(i)
     if head:
         head_reduce_upper()
+    reduce_last(1)
     reduce_last(0)
+    if head:
+        head_reduce_last()
     reduce_sent()
     out_copy.wait()
     din_copy.wait()
@@ -677,6 +705,7 @@
     DMA = pltpu.SemaphoreType.DMA
     across = DMA((PARTS, uppers - 1))
     inside = DMA((2, PARTS, e))
+    summed = DMA((len(reduce_waves(uppers)), PARTS, e))
     tops = DMA((uppers - 1 + e,))
     out, din, mine = pl.pallas_call(
         functools.partial(step_kernel, n, shard, slots, tok, tokp),
@@ -700,7 +729,7 @@
             VM((rows, 3 * D), BF), VM((slots * PAIRS, 2 * tokp, tokp), BF),
             VM((rows, D), BF),
             VM((rows, D), F32), VM((rows, 1), F32), VM((rows, D), F32), VM((rows, D), F32), VM((rows, D), BF),
-            DMA((4,)), across, across, inside, inside, across, across, inside, inside,
+            DMA((4,)), across, across, inside, inside, across, across, summed, summed,
             tops, tops, DMA((1,)), tops,
         ],
         compiler_params=pltpu.CompilerParams(

time: 127 us -> 112 us (0.88)
  Pallas kernels: 118 us -> 103 us
    pallas_call x1, Pallas kernels: 118 us -> 103 us  [run_step(): pl.pallas_call(functools.partial(step_kernel, n, shard, slots, tok, tokp)...]
where the time goes in v4:
time: 112 us; the launch traced here: 111 us
  Pallas kernels  103 us (92%)
  local copies, waits for them, and re-layouts  6.26 us (6%)
  between operations  1.33 us (1%)
  other arithmetic  1.16 us (1%)
    pallas_call x1, Pallas kernels, run_step(): pl.pallas_call(functools.partial(step_kernel, n, shard, slots, tok, tokp)...  103 us
    unnamed x4, local copies, waits for them, and re-layouts  3.55 us

profile of v4, /device:TPU:0, one launch (start us, length us, event | category | flops | bytes accessed | tf_op | source)
XLA Modules:
  0.0 111.4 jit_solution(15161548196498977603)
XLA Ops:
  1.3 1.0 pad.4
  2.3 1.2 %fusion.2.mine_ref = bf16[448,128]{1,0:T(8,128)(2,1)} fusion(s32[]{:T(128)S(6)} %select_n.24, bf16[57344]{0:T(1024)(128)(2,1)S(1)} %pad.4), kind=kLoop, calls=%fused_computation.4 | loop fusion | flops 229376 | bytes 229380 | tf_op jit(solution)/shard_map/reshape | solution.py:751
  3.4 102.7 %step.1 = (bf16[1576,384]{1,0:T(8,128)(2,1)}, bf16[1576,384]{1,0:T(8,128)(2,1)}, f32[448,128]{1,0:T(8,128)}) custom-call(s32[1]{0:T(128)S(6)} %copy.9.live_ref, bf16[448,128]{1,0:T(8,128)(2,1)} %fusion.2.mine_ref, bf16[1576,384]{1,0:T(8,128)(2,1)} %bitcast.17, bf16[1576,384]{1,0:T(8,128)(2,1)} %bitcast.18), custom_call_target="tpu_custom_call" | custom-call | tf_op jit(solution)/shard_map/step/pallas_call | solution.py:710
  106.1 1.8 %dynamic_slice.8 = f32[55440]{0:T(1024)} dynamic-slice(f32[57344]{0:T(1024)} %bitcast.19, s32[]{:T(128)S(6)} %select_n.25), dynamic_slice_sizes={55440} | dynamic-slice | bytes 443524 | tf_op jit(solution)/shard_map/dynamic_slice | solution.py:755
  107.9 0.0 copy-start
  107.9 2.5 %copy.10 = bf16[8,197,384]{2,0,1:T(8,128)(2,1)} copy(bf16[8,197,384]{2,0,1:T(8,128)(2,1)} %bitcast.16) | data formatting | bytes 2420736
  110.4 0.0 copy-done
  110.4 1.0 copy.11
Async XLA Ops:
  107.9 2.5 %copy-start = (bf16[1576,384]{1,0:T(8,128)(2,1)S(1)}, bf16[1576,384]{1,0:T(8,128)(2,1)}, u32[]{:S(2)}) copy-start(bf16[1576,384]{1,0:T(8,128)(2,1)} %get-tuple-element.7) | copy-start | bytes 3631108

commit v5 on v4

--- a/solution.py
+++ b/solution.py
@@ -258,8 +258,8 @@
             def _():
                 reduce_upper(p, j, to, peer(j)).start()
 
-    def reduce_round(i, wave):
-        for p in range(PARTS):
+    def reduce_round(i, wave, parts=range(PARTS)):
+        for p in parts:
             reduce_low(p, i, wave).wait_recv()
             keep = pl.ds(fixed(p, i), 1 << i)
             slot = pl.ds((1 << i) - 1, 1 << i)
@@ -367,10 +367,10 @@
         for c in range(3):
             buf[3 * r + c : 3 * r + c + 1, :] = value[:, c * LANES : (c + 1) * LANES]
 
-    def pack(blocks):
+    def pack(blocks, parts=range(PARTS)):
         for d in blocks:
             first = shard * d // LANES
-            for p in range(PARTS):
+            for p in parts:
                 at = first + p * part
                 gath[home(d, p)] = buf[at : at + part, :].astype(BF)
 
@@ -640,11 +640,35 @@
 
     lax.fori_loop(0, trips, backward, 0)
 
+    def grad_qkv(c, carry):
+        cols = pl.ds(pl.multiple_of(c * LANES, LANES), LANES)
+        grad = tn(attn_s[:, cols], qkv_s[...])
+        for b in range(9):
+            at = 3 * ROW_QKV + 9 * LANES * c + b
+            buf[pl.ds(at, LANES, 9), :] = grad[:, b * LANES : (b + 1) * LANES]
+        return carry
+
+    lax.fori_loop(0, 3, grad_qkv, 0)
+    for i in (BQ, BV):
+        put_vector(i, gvec[i : i + 1, :])
+    assert window // PARTS >= 6
+    later = range(1, PARTS)
+    pack(range(near_count))
+    for p in later:
+        reduce_low(p, e - 1, 0).start()
+    if head:
+        at = shard * near_count // LANES
+        head_v[...] = buf[at : at + 16, :].astype(BF)
+
     def first_norm_back(i, carry):
         for k in range(1, len(r_waves)):
-            @pl.when(i == 2 * (len(r_waves) - k) - 1)
+            @pl.when(i == len(r_waves) - 1 - k)
             def _():
                 reduce_round(0, k)
+
+        @pl.when(i == BLOCKS - 2)
+        def _():
+            reduce_round(e - 1, 0, later)
 
         rows = band(i)
         dn1 = nt(qkv_s[rows, :], wqkv[...])
@@ -656,27 +680,20 @@
 
     lax.fori_loop(0, BLOCKS, first_norm_back, 0)
 
-    def grad_qkv(c, carry):
-        cols = pl.ds(pl.multiple_of(c * LANES, LANES), LANES)
-        grad = tn(attn_s[:, cols], qkv_s[...])
-        for b in range(9):
-            at = 3 * ROW_QKV + 9 * LANES * c + b
-            buf[pl.ds(at, LANES, 9), :] = grad[:, b * LANES : (b + 1) * LANES]
-        return carry
-
-    lax.fori_loop(0, 3, grad_qkv, 0)
-    for i in (G1, S1, BQ, BV):
+    for i in (G1, S1):
         put_vector(i, gvec[i : i + 1, :])
-    send_blocks(0)
-    if head:
-        at = shard * near_count // LANES
-        head_v[...] = buf[at : at + 16, :].astype(BF)
+    pack(range(1), range(1))
+    reduce_low(0, e - 1, 0).start()
+    if e > 1:
+        reduce_round(e - 2, 0, later)
     gather_back(None, res_s)
     emit_rows(cot_v)
     din_copy = pltpu.make_async_copy(cot_v, din_ref, load_sem.at[3])
     din_copy.start()
     for i in reversed(range(e)):
-        reduce_round(i, 0)
+        reduce_round(i, 0, range(1))
+        if 1 < i + 1 < e:
+            reduce_round(i - 1, 0, later)
         if head:
             head_reduce_low(i)
     if head:

time: 112 us -> 110 us (0.982)
  Pallas kernels: 103 us -> 101 us
    pallas_call x1, Pallas kernels: 103 us -> 101 us  [run_step(): pl.pallas_call(functools.partial(step_kernel, n, shard, slots, tok, tokp)...]
where the time goes in v5:
time: 110 us
  Pallas kernels  101 us (92%)
  local copies, waits for them, and re-layouts  6.26 us (6%)
  between operations  1.33 us (1%)
  other arithmetic  1.16 us (1%)
    pallas_call x1, Pallas kernels, run_step(): pl.pallas_call(functools.partial(step_kernel, n, shard, slots, tok, tokp)...  101 us
    unnamed x4, local copies, waits for them, and re-layouts  3.55 us

profile of v5, /device:TPU:0, one launch (start us, length us, event | category | flops | bytes accessed | tf_op | source)
XLA Modules:
  0.0 109.8 jit_solution(3792035864174838594)
XLA Ops:
  1.3 1.0 pad.4
  2.3 1.2 %fusion.2.mine_ref = bf16[448,128]{1,0:T(8,128)(2,1)} fusion(s32[]{:T(128)S(6)} %select_n.24, bf16[57344]{0:T(1024)(128)(2,1)S(1)} %pad.4), kind=kLoop, calls=%fused_computation.4 | loop fusion | flops 229376 | bytes 229380 | tf_op jit(solution)/shard_map/reshape | solution.py:768
  3.4 101.0 %step.1 = (bf16[1576,384]{1,0:T(8,128)(2,1)}, bf16[1576,384]{1,0:T(8,128)(2,1)}, f32[448,128]{1,0:T(8,128)}) custom-call(s32[1]{0:T(128)S(6)} %copy.9.live_ref, bf16[448,128]{1,0:T(8,128)(2,1)} %fusion.2.mine_ref, bf16[1576,384]{1,0:T(8,128)(2,1)} %bitcast.17, bf16[1576,384]{1,0:T(8,128)(2,1)} %bitcast.18), custom_call_target="tpu_custom_call" | custom-call | tf_op jit(solution)/shard_map/step/pallas_call | solution.py:727
  104.5 1.8 %dynamic_slice.8 = f32[55440]{0:T(1024)} dynamic-slice(f32[57344]{0:T(1024)} %bitcast.19, s32[]{:T(128)S(6)} %select_n.25), dynamic_slice_sizes={55440} | dynamic-slice | bytes 443524 | tf_op jit(solution)/shard_map/dynamic_slice | solution.py:772
  106.2 0.0 copy-start
  106.2 2.5 %copy.10 = bf16[8,197,384]{2,0,1:T(8,128)(2,1)} copy(bf16[8,197,384]{2,0,1:T(8,128)(2,1)} %bitcast.16) | data formatting | bytes 2420736
  108.8 0.0 copy-done
  108.8 1.0 copy.11
Async XLA Ops:
  106.2 2.5 %copy-start = (bf16[1576,384]{1,0:T(8,128)(2,1)S(1)}, bf16[1576,384]{1,0:T(8,128)(2,1)}, u32[]{:S(2)}) copy-start(bf16[1576,384]{1,0:T(8,128)(2,1)} %get-tuple-element.7) | copy-start | bytes 3631108
